TPU v7x, 768 devices: a whole 4x8x12 slice. The times are simulated.
768 devices in a mesh: row: 192 (over y_hi, x, z), col: 4 (over y_lo, core).
Axes of the slice: x: 4, y: 8 (y_hi: 4, y_lo: 2; y = y_hi * 2 + y_lo), z: 12, core: 2. Of those that a mesh axis runs over, the one named last changes fastest.
Arguments:
- features: bfloat16 [49152, 256], P('row', 'col'), may hold values from -6 to 6
- weight: bfloat16 [256, 256], P(None, 'col'), may hold values from -1.5 to 1.5
- bias: float32 [256], P('col'), may hold values from -3 to 3
- adjacency: bfloat16 [384, 32, 128, 128], P('row'), may hold values from 0 to 1.5, as said below
- block_cols: int32 [384, 32], P('row'), may hold values from 0 to 383, as said below
- block_count: int32 [384], P('row'), may hold values from 2 to 32
Outputs:
- hidden_out: bfloat16 [49152, 256], P('row', 'col')
Inputs may be any that keep to these rules, and one draw needn't show every extreme that they name: `adjacency`: about two nonzero entries a row in each stored block on average; nonzero entries lie between 0.5 and 1.5. `block_cols`: slot 0 of block row r names block r; slot 1 names its paired block (r + 192) mod 384; every other entry lies within 2 blocks of r; entries may repeat.
All inputs are finite; a program needn't handle non-finite values.
Results may differ from a plain program's by a relative error of at most 0.0085.
Values may be sent and summed in bfloat16 or wider, within the bound.
No kernel may reach another device: no remote copies, remote signals or barrier semaphores. Data moves between devices by JAX's collectives and lax.ppermute only.
A program may use at most 32 MiB of HBM per device.

v0:
```python
import jax
import jax.numpy as jnp
from jax import lax
from jax.sharding import PartitionSpec as P


def aggregate(tiles, cols, alive, gathered):
    bsize = tiles.shape[2]
    blocks = gathered.reshape(gathered.shape[0] // bsize, bsize, gathered.shape[1])
    picked = blocks[cols]
    summed = jnp.einsum(
        "rkij,rkjf,rk->rif", tiles, picked, alive, preferred_element_type=jnp.float32
    )
    return summed.reshape(tiles.shape[0] * bsize, gathered.shape[1])


def on_device(features, weight, bias, adjacency, block_cols, block_count):
    kmax = adjacency.shape[1]
    full_in = lax.all_gather(features, "col", axis=1, tiled=True)
    alive = (jnp.arange(kmax, dtype=jnp.int32)[None, :] < block_count[:, None]).astype(jnp.bfloat16)
    degree = 1.0 + jnp.einsum(
        "rkij,rk->ri", adjacency, alive, preferred_element_type=jnp.float32
    ).reshape(-1)
    scale = lax.rsqrt(degree)
    own_panel = (
        jnp.dot(full_in, weight, preferred_element_type=jnp.float32) * scale[:, None]
    ).astype(jnp.bfloat16)
    gathered = lax.all_gather(own_panel, "row", axis=0, tiled=True)
    agg = aggregate(adjacency, block_cols, alive, gathered)
    result = jax.nn.relu(scale[:, None] * (agg + own_panel.astype(jnp.float32)) + bias[None, :])
    return result.astype(jnp.bfloat16)


def solution(mesh):
    return jax.shard_map(
        on_device,
        mesh=mesh,
        in_specs=(
            P("row", "col"),
            P(None, "col"),
            P("col"),
            P("row", None, None, None),
            P("row", None),
            P("row"),
        ),
        out_specs=P("row", "col"),
        check_vma=False,
    )
```

profile of v0, /device:TPU:56, one launch (start us, length us, event | category | flops | bytes accessed | tf_op | source)
XLA Modules:
  0.0 226.9 jit_solution(1365353442613652748)
XLA Ops:
  6.5 0.0 copy-start
  6.5 0.0 copy-start.3
  6.5 0.0 copy-start.4
  6.5 0.0 all-gather.2.cloned.1.call-start
  6.5 0.7 fusion.10
  7.3 2.2 convert_reduce_fusion
  9.5 0.1 fusion.8
  9.6 0.0 copy-done.3
  9.6 5.4 %all_gather.6 = bf16[256,256]{0,1:T(8,128)(2,1)S(1)} all-gather(bf16[256,64]{0,1:T(8,128)(2,1)S(1)} %copy-done.3), channel_id=1, replica_groups=mesh['row'=192,'col'=4] {'col'}, dimensions={1}, use_global_device_ids=true | all-gather | bytes 163840 | tf_op jit(solution)/shard_map/all_gather | solution.py:19
  15.1 0.0 copy-done
  15.1 0.8 fusion.2
  15.8 0.0 all-gather.2.cloned.1.call-update
  15.9 0.0 copy-done.4
  15.9 0.1 reshape.22
  16.0 191.5 %all-gather.2.cloned.1.call-done = bf16[49152,64]{0,1:T(8,128)(2,1)} async-done(((bf16[256,64]{0,1:T(8,128)(2,1)}), bf16[49152,64]{0,1:T(8,128)(2,1)}) %all-gather.2.cloned.1.call-update) | async-done | bytes 6291472 | tf_op jit(solution)/shard_map/all_gather | solution.py:28
  207.5 7.2 %copy_bitcast_fusion = bf16[384,128,64]{1,2,0:T(8,128)(2,1)} fusion(bf16[49152,64]{0,1:T(8,128)(2,1)} %all-gather.2.cloned.1.call-done), kind=kLoop, calls=%fused_computation.1 | loop fusion | bytes 12582912 | tf_op jit(solution)/shard_map/reshape | solution.py:9
  214.7 0.0 copy-start.1
  214.7 3.7 %gather_fusion = bf16[64,128,64]{1,2,0:T(8,128)(2,1)S(1)} fusion(bf16[384,128,64]{1,2,0:T(8,128)(2,1)} %copy_bitcast_fusion, s32[1024]{0:T(1024)S(1)} %pad_clamp_fusion), kind=kCustom, calls=%fused_computation | custom fusion | bytes 2097408 | tf_op jit(solution)/shard_map/gather | solution.py:10
  218.4 0.0 copy-start.2
  218.4 0.0 copy-start.5
  218.4 0.0 copy-done.1
  218.4 0.9 fusion.1
  219.3 0.0 copy-done.2
  219.3 0.0 copy-done.5
  219.3 0.7 fusion.7
  (3 shorter events, 0.0 us)
Async XLA Ops:
  6.5 8.5 %copy-start = (bf16[256,64]{0,1:T(8,128)(2,1)S(1)}, bf16[256,64]{0,1:T(8,128)(2,1)}, u32[]{:S(2)}) copy-start(bf16[256,64]{0,1:T(8,128)(2,1)} %param.7) | copy-start | bytes 98308
  6.5 3.1 %copy-start.3 = (bf16[256,64]{0,1:T(8,128)(2,1)S(1)}, bf16[256,64]{0,1:T(8,128)(2,1)}, u32[]{:S(2)}) copy-start(bf16[256,64]{0,1:T(8,128)(2,1)} %param.6) | copy-start | bytes 98308
  6.5 9.3 %copy-start.4 = (s32[2,32]{1,0:T(2,128)S(1)}, s32[2,32]{1,0:T(2,128)}, u32[]{:S(2)}) copy-start(s32[2,32]{1,0:T(2,128)} %param.10) | copy-start | bytes 772
  6.5 200.9 %all-gather.2.cloned.1.call-start = ((), (), s32[]{:S(2)}) async-start(), calls=%async_computation | async-start | bytes 6324224 | tf_op jit(solution)/shard_map/all_gather | solution.py:28
  214.7 3.7 %copy-start.1 = (bf16[2,32,128,128]{3,2,1,0:T(8,128)(2,1)S(1)}, bf16[2,32,128,128]{3,2,1,0:T(8,128)(2,1)}, u32[]{:S(2)}) copy-start(bf16[2,32,128,128]{3,2,1,0:T(8,128)(2,1)} %param.9) | copy-start | bytes 6291460
  218.4 0.9 copy-start.2
  218.4 0.9 copy-start.5
Sparse Core Ops, SparseCore 0:
  16.0 191.4 all-gather.1
where the time goes:
time: 229 us; the launch traced here: 227 us
  waiting for transfers between devices  192 us (84%)
  between operations  13.5 us (6%)
  local copies, waits for them, and re-layouts  11 us (5%)
  blocking collectives  5.42 us (2%)
  other arithmetic  3.67 us (2%)
    all_gather x1, waiting for transfers between devices, on_device(): gathered = lax.all_gather(own_panel, 'row', axis=0, tiled=True)  192 us
    reshape x1, local copies, waits for them, and re-layouts, aggregate(): gathered.reshape(gathered.shape[0] // bsize, bsize, gathered.shape[1])  7.23 us
    all_gather x1, blocking collectives, on_device(): full_in = lax.all_gather(features, 'col', axis=1, tiled=True)  5.42 us
  transfers between devices with their start and end apart: 1, of which 1 were waited for; matrix products, arithmetic and copies ran while one was open for 0% of the time, Pallas kernels for 0%

commit v1 on v0

v1 whole, which is shorter than its diff:
```python
import jax
import jax.numpy as jnp
from jax import lax
from jax.experimental import pallas as pl
from jax.experimental.pallas import tpu as pltpu
from jax.sharding import PartitionSpec as P

F32 = jnp.float32
BF16 = jnp.bfloat16
SMEM = pltpu.MemorySpace.SMEM
VMEM = pltpu.MemorySpace.VMEM
NT = (((1,), (1,)), ((), ()))


def split(value):
    high = value.astype(BF16)
    return high, (value - high.astype(F32)).astype(BF16)


def degree_kernel(count_ref, feat_ref, adj_ref, out_ref, tiles, sums, sem):
    kmax, part, lanes = tiles.shape
    bsize = adj_ref.shape[2]
    col = lax.axis_index("col")
    start = col * part
    r = start // bsize
    offset = pl.multiple_of(lax.rem(start, bsize), part)
    copy = pltpu.make_async_copy(adj_ref.at[r, :, pl.ds(offset, part), :], tiles, sem)
    copy.start()
    rows = feat_ref.shape[0]
    out_ref[:rows, :] = feat_ref[...]
    sums[...] = jnp.zeros_like(sums)
    count = count_ref[r]
    copy.wait()
    total = jnp.zeros((part, lanes), F32)
    for k in range(kmax):
        total += jnp.where(k < count, tiles[k].astype(F32), 0.0)
    total_at = pl.multiple_of(start, part)
    sums[pl.ds(total_at, part), :] = total
    ones = jnp.ones((16, lanes), BF16)
    high, low = split(sums[...])
    degree = 1.0 + (
        lax.dot_general(ones, high, NT, preferred_element_type=F32)
        + lax.dot_general(ones, low, NT, preferred_element_type=F32)
    )
    nodes = degree.shape[1]
    node = lax.broadcasted_iota(jnp.int32, degree.shape, 1)
    row = lax.broadcasted_iota(jnp.int32, degree.shape, 0)
    scale = lax.rsqrt(degree)
    scale = jnp.where((node >= start) & (node < start + part), scale, 0.0)
    high = scale.astype(BF16).astype(F32)
    tail = jnp.where(row == 0, high, jnp.where(row == 1, scale - high, 0.0))
    out_ref[rows:, :] = tail.astype(BF16)


def transform_kernel(gathered_ref, weight_ref, z_ref, scale_ref):
    panels = gathered_ref.shape[0]
    rows = weight_ref.shape[0]
    features = weight_ref.shape[1] // panels
    full = jnp.concatenate([gathered_ref[c, :features, :] for c in range(panels)], axis=0)
    scale = jnp.zeros((1, full.shape[1]), F32)
    for c in range(panels):
        scale += gathered_ref[c, features : features + 1, :].astype(F32)
        scale += gathered_ref[c, features + 1 : features + 2, :].astype(F32)
    product = jnp.dot(weight_ref[...], full, preferred_element_type=F32)
    z_ref[...] = (product * scale).astype(BF16)
    scale_ref[...] = jnp.broadcast_to(scale, scale_ref.shape)


def blocks_kernel(nblk, count_ref, cols_ref, tiles, z_ref, bias_ref, near_ref, base_ref, offset_ref, acc):
    own_rows, _, bsize, _ = tiles.shape
    first = lax.axis_index("row") * own_rows - 2
    acc[...] = jnp.zeros_like(acc)
    features = bias_ref.shape[1]
    eye = lax.broadcasted_iota(jnp.int32, (features, features), 0) == lax.broadcasted_iota(
        jnp.int32, (features, features), 1
    )
    offset_ref[...] = jnp.sum(jnp.where(eye, bias_ref[...], 0.0), axis=1, keepdims=True)
    for r in range(own_rows):
        rows = slice(r * bsize, (r + 1) * bsize)
        acc[6 + r, rows, :] = tiles[r, 1].astype(F32)

        def step(k, _):
            place = lax.rem(cols_ref[r, k] - first + 2 * nblk, nblk)
            place = jnp.clip(place, 0, 5)
            acc[place, rows, :] += tiles[r, k].astype(F32)
            return 0

        step(0, 0)
        lax.fori_loop(2, count_ref[r], step, 0)
    for slot, pair in enumerate((0, 4, 6)):
        for h in range(2):
            near_ref[slot, :, h * bsize : (h + 1) * bsize] = acc[pair + h].astype(BF16)
    own = jnp.concatenate([acc[2].astype(BF16), acc[3].astype(BF16)], axis=1)
    z = z_ref[...]
    base_ref[...] = z.astype(F32) + lax.dot_general(z, own, NT, preferred_element_type=F32)


def finish_kernel(before_ref, after_ref, pair_ref, near_ref, base_ref, scale_ref, offset_ref, out_ref):
    total = base_ref[...]
    for slot, ref in enumerate((before_ref, after_ref, pair_ref)):
        total += lax.dot_general(ref[...], near_ref[slot], NT, preferred_element_type=F32)
    result = scale_ref[:1, :] * total + offset_ref[...]
    out_ref[...] = jnp.maximum(result, 0.0).astype(BF16)


def on_device(features, weight, bias, adjacency, block_cols, block_count):
    own_rows, kmax, bsize, _ = adjacency.shape
    devices = lax.axis_size("row")
    panels = lax.axis_size("col")
    nblk = devices * own_rows
    nodes, width = features.shape
    outs = weight.shape[1]
    part = nodes // panels
    vmem = pl.BlockSpec(memory_space=VMEM)
    smem = pl.BlockSpec(memory_space=SMEM)
    hbm = pl.BlockSpec(memory_space=pltpu.MemorySpace.HBM)

    sent = pl.pallas_call(
        degree_kernel,
        out_shape=jax.ShapeDtypeStruct((width + 16, nodes), BF16),
        in_specs=[smem, vmem, hbm],
        out_specs=vmem,
        scratch_shapes=[
            pltpu.VMEM((kmax, part, bsize), BF16),
            pltpu.VMEM((nodes, bsize), F32),
            pltpu.SemaphoreType.DMA,
        ],
        compiler_params=pltpu.CompilerParams(vmem_limit_bytes=4 << 20),
        name="degree",
    )(block_count, features.T, adjacency)
    gathered = lax.all_gather(sent, "col", axis=0, tiled=False)
    z, scale = pl.pallas_call(
        transform_kernel,
        out_shape=(
            jax.ShapeDtypeStruct((outs, nodes), BF16),
            jax.ShapeDtypeStruct((8, nodes), F32),
        ),
        in_specs=[vmem, vmem],
        out_specs=(vmem, vmem),
        compiler_params=pltpu.CompilerParams(vmem_limit_bytes=4 << 20),
        name="transform",
    )(gathered, weight.T)

    def shift(step):
        return lax.ppermute(z, "row", [(s, (s + step) % devices) for s in range(devices)])

    pair, before, after = shift(devices // 2), shift(1), shift(-1)
    near, base, offset = pl.pallas_call(
        lambda *refs: blocks_kernel(nblk, *refs),
        out_shape=(
            jax.ShapeDtypeStruct((3, nodes, 2 * bsize), BF16),
            jax.ShapeDtypeStruct((outs, nodes), F32),
            jax.ShapeDtypeStruct((outs, 1), F32),
        ),
        in_specs=[smem, smem, vmem, vmem, vmem],
        out_specs=(vmem, vmem, vmem),
        scratch_shapes=[pltpu.VMEM((8, nodes, bsize), F32)],
        cost_estimate=pl.CostEstimate(flops=70_000_000, bytes_accessed=2_500_000, transcendentals=0),
        compiler_params=pltpu.CompilerParams(vmem_limit_bytes=12 << 20),
        name="blocks",
    )(block_count, block_cols, adjacency, z, bias.reshape(1, -1))
    out = pl.pallas_call(
        finish_kernel,
        out_shape=jax.ShapeDtypeStruct((outs, nodes), BF16),
        in_specs=[vmem] * 7,
        out_specs=vmem,
        compiler_params=pltpu.CompilerParams(vmem_limit_bytes=4 << 20),
        name="finish",
    )(before, after, pair, near, base, scale, offset)
    return out.T


def solution(mesh):
    return jax.shard_map(
        on_device,
        mesh=mesh,
        in_specs=(
            P("row", "col"),
            P(None, "col"),
            P("col"),
            P("row", None, None, None),
            P("row", None),
            P("row"),
        ),
        out_specs=P("row", "col"),
        check_vma=False,
    )
```

time: 229 us -> 47.5 us (0.21)
  the two profiles are of different devices: /device:TPU:56 before, /device:TPU:8 now
where the time goes in v1:
time: 47.5 us; the launch traced here: 47.2 us
  starting transfers between devices  18.5 us (39%)
  blocking collectives  13.2 us (28%)
  waiting for transfers between devices  9.35 us (20%)
  local copies, waits for them, and re-layouts  3.05 us (6%)
  Pallas kernels  2.99 us (6%)
    ppermute x3, starting transfers between devices, shift(): lax.ppermute(z, 'row', [(s, (s + step) % devices) for s in range(devices)])  18.5 us
    all_gather x1, blocking collectives, on_device(): gathered = lax.all_gather(sent, 'col', axis=0, tiled=False)  13.2 us
    ppermute x3, waiting for transfers between devices, shift(): lax.ppermute(z, 'row', [(s, (s + step) % devices) for s in range(devices)])  9.35 us
    unnamed x16, local copies, waits for them, and re-layouts  3.05 us
    pallas_call x1, Pallas kernels, on_device(): pl.pallas_call(lambda *refs: blocks_kernel(nblk, *refs), out_shape=(jax.S...  1.04 us
  transfers between devices with their start and end apart: 3, of which 1 were waited for; matrix products, arithmetic and copies ran while one was open for 0% of the time, Pallas kernels for 2%

profile of v1, /device:TPU:8, one launch (start us, length us, event | category | flops | bytes accessed | tf_op | source)
XLA Modules:
  0.0 47.2 jit_solution(12314220999853080467)
XLA Ops:
  0.0 0.0 copy-start.5
  0.0 0.0 copy-start.6
  0.0 0.0 copy-start
  0.0 1.6 %copy-done = bf16[2,32,128,128]{3,2,1,0:T(8,128)(2,1)S(1)} copy-done((bf16[2,32,128,128]{3,2,1,0:T(8,128)(2,1)S(1)}, bf16[2,32,128,128]{3,2,1,0:T(8,128)(2,1)}, u32[]{:S(2)}) %copy-start) | copy-done | bytes 2097176
  1.6 0.0 copy-start.2
  1.6 0.8 %copy-done.2 = bf16[256,64]{0,1:T(8,128)(2,1)S(1)} copy-done((bf16[256,64]{0,1:T(8,128)(2,1)S(1)}, bf16[256,64]{0,1:T(8,128)(2,1)}, u32[]{:S(2)}) %copy-start.2) | copy-done | bytes 32792
  2.4 0.0 copy-start.4
  2.4 0.7 %copy-done.4 = s32[2]{0:T(128)S(1)} copy-done((s32[2]{0:T(128)S(1)}, s32[2]{0:T(128)}, u32[]{:S(2)}) %copy-start.4) | copy-done | bytes 32
  3.0 0.0 copy-start.3
  3.0 0.0 copy-start.1
  3.0 0.0 copy-start.7
  3.0 0.9 %degree.1 = bf16[80,256]{1,0:T(8,128)(2,1)S(1)} custom-call(s32[2]{0:T(128)S(1)} %copy-done.4, bf16[64,256]{1,0:T(8,128)(2,1)S(1)} %bitcast.6, bf16[2,32,128,128]{3,2,1,0:T(8,128)(2,1)S(1)} %copy-done), custom_call_target="tpu_custom_call" | custom-call | tf_op jit(solution)/shard_map/degree/pallas_call | solution.py:118
  4.0 13.2 %all-gather = bf16[320,256]{1,0:T(8,128)(2,1)S(1)} all-gather(bf16[80,256]{1,0:T(8,128)(2,1)S(1)} %degree.1), channel_id=2, replica_groups=mesh['row'=192,'col'=4] {'col'}, dimensions={0}, use_global_device_ids=true | all-gather | bytes 204800 | tf_op jit(solution)/shard_map/all_gather | solution.py:131
  17.2 0.0 copy-done.3
  17.2 0.1 transform.1
  17.3 1.9 %collective-permute-start.2 = (bf16[64,256]{1,0:T(8,128)(2,1)S(1)}, bf16[64,256]{1,0:T(8,128)(2,1)S(1)}, u32[]{:S(2)}, u32[]{:S(2)}) collective-permute-start(bf16[64,256]{1,0:T(8,128)(2,1)S(1)} %get-tuple-element.10.refs_3_), channel_id=1, source_target_pairs={{0,384},{4,388},{8,392},{12,396},{16,400},{20,404},{24,408},{28,41... | collective-permute-start | bytes 98312 | tf_op jit(solution)/shard_map/ppermute | solution.py:145
  19.2 14.7 %collective-permute-start.1 = (bf16[64,256]{1,0:T(8,128)(2,1)S(1)}, bf16[64,256]{1,0:T(8,128)(2,1)S(1)}, u32[]{:S(2)}, u32[]{:S(2)}) collective-permute-start(bf16[64,256]{1,0:T(8,128)(2,1)S(1)} %get-tuple-element.10.refs_3_), channel_id=1, source_target_pairs={{0,764},{4,0},{8,4},{12,8},{16,12},{20,16},{24,20},{28,24},{32,28}... | collective-permute-start | bytes 98312 | tf_op jit(solution)/shard_map/ppermute | solution.py:145
  33.9 1.9 %collective-permute-start = (bf16[64,256]{1,0:T(8,128)(2,1)S(1)}, bf16[64,256]{1,0:T(8,128)(2,1)S(1)}, u32[]{:S(2)}, u32[]{:S(2)}) collective-permute-start(bf16[64,256]{1,0:T(8,128)(2,1)S(1)} %get-tuple-element.10.refs_3_), channel_id=1, source_target_pairs={{0,4},{4,8},{8,12},{12,16},{16,20},{20,24},{24,28},{28,32},{32,36}... | collective-permute-start | bytes 98312 | tf_op jit(solution)/shard_map/ppermute | solution.py:145
  35.9 0.0 copy-done.5
  35.9 0.0 copy-done.6
  35.9 0.0 copy-done.1
  35.9 0.0 copy-done.7
  35.9 1.0 %blocks.1 = (bf16[3,256,256]{2,1,0:T(8,128)(2,1)S(1)}, f32[64,256]{1,0:T(8,128)S(1)}, f32[64,1]{1,0:T(8,128)S(1)}) custom-call(s32[2]{0:T(128)S(1)} %copy-done.5, s32[2,32]{1,0:T(2,128)S(1)} %copy-done.6, bf16[2,32,128,128]{3,2,1,0:T(8,128)(2,1)S(1)} %copy-done.1, bf16[64,256]{1,0:T(8,128)(2,1)S(1)} %get-tuple-element.10.refs_3_, f32[1,64]{1,0:T(1,128)S(1)} %bitcast.8), custom_call_target="tpu_custom_call" | custom-call | flops 70000000 | bytes 2500000 | tf_op jit(solution)/shard_map/blocks/pallas_call | solution.py:148
  36.9 0.0 collective-permute-done.2.pair_ref
  37.0 0.0 collective-permute-done.1.after_ref
  37.0 9.3 %collective-permute-done.before_ref = bf16[64,256]{1,0:T(8,128)(2,1)S(1)} collective-permute-done((bf16[64,256]{1,0:T(8,128)(2,1)S(1)}, bf16[64,256]{1,0:T(8,128)(2,1)S(1)}, u32[]{:S(2)}, u32[]{:S(2)}) %collective-permute-start) | collective-permute-done | bytes 32800 | tf_op jit(solution)/shard_map/ppermute | solution.py:145
  46.3 0.9 %finish.1 = bf16[64,256]{1,0:T(8,128)(2,1)} custom-call(bf16[64,256]{1,0:T(8,128)(2,1)S(1)} %collective-permute-done.before_ref, bf16[64,256]{1,0:T(8,128)(2,1)S(1)} %collective-permute-done.1.after_ref, bf16[64,256]{1,0:T(8,128)(2,1)S(1)} %collective-permute-done.2.pair_ref, bf16[3,256,256]{2,1,0:T(8,128)(2,1)S(1)} %get-tuple-element.11.near_ref, ...), custom_call_target="tpu_custom_call" | custom-call | tf_op jit(solution)/shard_map/finish/pallas_call | solution.py:162
Async XLA Ops:
  0.0 35.9 %copy-start.5 = (s32[2]{0:T(128)S(1)}, s32[2]{0:T(128)}, u32[]{:S(2)}) copy-start(s32[2]{0:T(128)} %refs_0_.1) | copy-start | bytes 28
  0.0 35.9 %copy-start.6 = (s32[2,32]{1,0:T(2,128)S(1)}, s32[2,32]{1,0:T(2,128)}, u32[]{:S(2)}) copy-start(s32[2,32]{1,0:T(2,128)} %refs_1_.1) | copy-start | bytes 772
  0.0 1.6 %copy-start = (bf16[2,32,128,128]{3,2,1,0:T(8,128)(2,1)S(1)}, bf16[2,32,128,128]{3,2,1,0:T(8,128)(2,1)}, u32[]{:S(2)}) copy-start(bf16[2,32,128,128]{3,2,1,0:T(8,128)(2,1)} %refs_2_.1) | copy-start | bytes 6291460
  1.6 0.8 %copy-start.2 = (bf16[256,64]{0,1:T(8,128)(2,1)S(1)}, bf16[256,64]{0,1:T(8,128)(2,1)}, u32[]{:S(2)}) copy-start(bf16[256,64]{0,1:T(8,128)(2,1)} %param.6) | copy-start | bytes 98308
  2.4 0.7 %copy-start.4 = (s32[2]{0:T(128)S(1)}, s32[2]{0:T(128)}, u32[]{:S(2)}) copy-start(s32[2]{0:T(128)} %refs_0_.1) | copy-start | bytes 28
  3.0 14.1 %copy-start.3 = (bf16[256,64]{0,1:T(8,128)(2,1)S(1)}, bf16[256,64]{0,1:T(8,128)(2,1)}, u32[]{:S(2)}) copy-start(bf16[256,64]{0,1:T(8,128)(2,1)} %param.7) | copy-start | bytes 98308
  3.0 32.9 %copy-start.1 = (bf16[2,32,128,128]{3,2,1,0:T(8,128)(2,1)S(1)}, bf16[2,32,128,128]{3,2,1,0:T(8,128)(2,1)}, u32[]{:S(2)}) copy-start(bf16[2,32,128,128]{3,2,1,0:T(8,128)(2,1)} %refs_2_.1) | copy-start | bytes 6291460
  3.0 32.9 %copy-start.7 = (f32[64]{0:T(128)S(1)}, f32[64]{0:T(128)}, u32[]{:S(2)}) copy-start(f32[64]{0:T(128)} %param.8) | copy-start | bytes 772
  17.3 19.7 %collective-permute-start.2 = (bf16[64,256]{1,0:T(8,128)(2,1)S(1)}, bf16[64,256]{1,0:T(8,128)(2,1)S(1)}, u32[]{:S(2)}, u32[]{:S(2)}) collective-permute-start(bf16[64,256]{1,0:T(8,128)(2,1)S(1)} %get-tuple-element.10.refs_3_), channel_id=1, source_target_pairs={{0,384},{4,388},{8,392},{12,396},{16,400},{20,404},{24,408},{28,41... | collective-permute-start | bytes 98312 | tf_op jit(solution)/shard_map/ppermute | solution.py:145
  19.2 17.8 %collective-permute-start.1 = (bf16[64,256]{1,0:T(8,128)(2,1)S(1)}, bf16[64,256]{1,0:T(8,128)(2,1)S(1)}, u32[]{:S(2)}, u32[]{:S(2)}) collective-permute-start(bf16[64,256]{1,0:T(8,128)(2,1)S(1)} %get-tuple-element.10.refs_3_), channel_id=1, source_target_pairs={{0,764},{4,0},{8,4},{12,8},{16,12},{20,16},{24,20},{28,24},{32,28}... | collective-permute-start | bytes 98312 | tf_op jit(solution)/shard_map/ppermute | solution.py:145
  33.9 12.4 %collective-permute-start = (bf16[64,256]{1,0:T(8,128)(2,1)S(1)}, bf16[64,256]{1,0:T(8,128)(2,1)S(1)}, u32[]{:S(2)}, u32[]{:S(2)}) collective-permute-start(bf16[64,256]{1,0:T(8,128)(2,1)S(1)} %get-tuple-element.10.refs_3_), channel_id=1, source_target_pairs={{0,4},{4,8},{8,12},{12,16},{16,20},{20,24},{24,28},{28,32},{32,36}... | collective-permute-start | bytes 98312 | tf_op jit(solution)/shard_map/ppermute | solution.py:145

commit v2 on v1

--- a/solution.py
+++ b/solution.py
@@ -10,6 +10,7 @@
 SMEM = pltpu.MemorySpace.SMEM
 VMEM = pltpu.MemorySpace.VMEM
 NT = (((1,), (1,)), ((), ()))
+LINE = 12
 
 
 def split(value):
@@ -17,32 +18,38 @@
     return high, (value - high.astype(F32)).astype(BF16)
 
 
-def degree_kernel(count_ref, feat_ref, adj_ref, out_ref, tiles, sums, sem):
+def degree_kernel(count_hbm, feat_hbm, adj_hbm, out_ref, counts, tiles, sums, sems):
     kmax, part, lanes = tiles.shape
-    bsize = adj_ref.shape[2]
-    col = lax.axis_index("col")
-    start = col * part
+    bsize = adj_hbm.shape[2]
+    rows = feat_hbm.shape[0]
+    start = lax.axis_index("col") * part
     r = start // bsize
     offset = pl.multiple_of(lax.rem(start, bsize), part)
-    copy = pltpu.make_async_copy(adj_ref.at[r, :, pl.ds(offset, part), :], tiles, sem)
-    copy.start()
-    rows = feat_ref.shape[0]
-    out_ref[:rows, :] = feat_ref[...]
+    half = kmax // 2
+    loads = [pltpu.make_async_copy(count_hbm, counts, sems.at[0])]
+    for h in range(2):
+        ks = pl.ds(h * half, half)
+        loads.append(
+            pltpu.make_async_copy(adj_hbm.at[r, ks, pl.ds(offset, part), :], tiles.at[ks], sems.at[1 + h])
+        )
+    loads.append(pltpu.make_async_copy(feat_hbm, out_ref.at[pl.ds(0, rows), :], sems.at[3]))
+    for load in loads:
+        load.start()
     sums[...] = jnp.zeros_like(sums)
-    count = count_ref[r]
-    copy.wait()
+    loads[0].wait()
+    count = counts[r]
     total = jnp.zeros((part, lanes), F32)
-    for k in range(kmax):
-        total += jnp.where(k < count, tiles[k].astype(F32), 0.0)
-    total_at = pl.multiple_of(start, part)
-    sums[pl.ds(total_at, part), :] = total
+    for h in range(2):
+        loads[1 + h].wait()
+        for k in range(h * half, (h + 1) * half):
+            total += jnp.where(k < count, tiles[k].astype(F32), 0.0)
+    sums[pl.ds(pl.multiple_of(start, part), part), :] = total
     ones = jnp.ones((16, lanes), BF16)
     high, low = split(sums[...])
     degree = 1.0 + (
         lax.dot_general(ones, high, NT, preferred_element_type=F32)
         + lax.dot_general(ones, low, NT, preferred_element_type=F32)
     )
-    nodes = degree.shape[1]
     node = lax.broadcasted_iota(jnp.int32, degree.shape, 1)
     row = lax.broadcasted_iota(jnp.int32, degree.shape, 0)
     scale = lax.rsqrt(degree)
@@ -50,6 +57,7 @@
     high = scale.astype(BF16).astype(F32)
     tail = jnp.where(row == 0, high, jnp.where(row == 1, scale - high, 0.0))
     out_ref[rows:, :] = tail.astype(BF16)
+    loads[3].wait()
 
 
 def transform_kernel(gathered_ref, weight_ref, z_ref, scale_ref):
@@ -66,7 +74,7 @@
     scale_ref[...] = jnp.broadcast_to(scale, scale_ref.shape)
 
 
-def blocks_kernel(nblk, count_ref, cols_ref, tiles, z_ref, bias_ref, near_ref, base_ref, offset_ref, acc):
+def blocks_kernel(count_ref, cols_ref, tiles, z_ref, bias_ref, near_ref, base_ref, offset_ref, same_ref, acc):
     own_rows, _, bsize, _ = tiles.shape
     first = lax.axis_index("row") * own_rows - 2
     acc[...] = jnp.zeros_like(acc)
@@ -80,8 +88,7 @@
         acc[6 + r, rows, :] = tiles[r, 1].astype(F32)
 
         def step(k, _):
-            place = lax.rem(cols_ref[r, k] - first + 2 * nblk, nblk)
-            place = jnp.clip(place, 0, 5)
+            place = jnp.clip(cols_ref[r, k] - first, 0, 5)
             acc[place, rows, :] += tiles[r, k].astype(F32)
             return 0
 
@@ -92,13 +99,16 @@
             near_ref[slot, :, h * bsize : (h + 1) * bsize] = acc[pair + h].astype(BF16)
     own = jnp.concatenate([acc[2].astype(BF16), acc[3].astype(BF16)], axis=1)
     z = z_ref[...]
+    same_ref[...] = z
     base_ref[...] = z.astype(F32) + lax.dot_general(z, own, NT, preferred_element_type=F32)
 
 
-def finish_kernel(before_ref, after_ref, pair_ref, near_ref, base_ref, scale_ref, offset_ref, out_ref):
+def finish_kernel(
+    after_ref, before_ref, first_ref, last_ref, near_ref, base_ref, scale_ref, offset_ref, out_ref
+):
     total = base_ref[...]
-    for slot, ref in enumerate((before_ref, after_ref, pair_ref)):
-        total += lax.dot_general(ref[...], near_ref[slot], NT, preferred_element_type=F32)
+    for slot, z in enumerate((before_ref[...], after_ref[...], first_ref[...] + last_ref[...])):
+        total += lax.dot_general(z, near_ref[slot], NT, preferred_element_type=F32)
     result = scale_ref[:1, :] * total + offset_ref[...]
     out_ref[...] = jnp.maximum(result, 0.0).astype(BF16)
 
@@ -107,7 +117,6 @@
     own_rows, kmax, bsize, _ = adjacency.shape
     devices = lax.axis_size("row")
     panels = lax.axis_size("col")
-    nblk = devices * own_rows
     nodes, width = features.shape
     outs = weight.shape[1]
     part = nodes // panels
@@ -118,14 +127,15 @@
     sent = pl.pallas_call(
         degree_kernel,
         out_shape=jax.ShapeDtypeStruct((width + 16, nodes), BF16),
-        in_specs=[smem, vmem, hbm],
+        in_specs=[hbm, hbm, hbm],
         out_specs=vmem,
         scratch_shapes=[
+            pltpu.SMEM((own_rows,), jnp.int32),
             pltpu.VMEM((kmax, part, bsize), BF16),
             pltpu.VMEM((nodes, bsize), F32),
-            pltpu.SemaphoreType.DMA,
+            pltpu.SemaphoreType.DMA((4,)),
         ],
-        compiler_params=pltpu.CompilerParams(vmem_limit_bytes=4 << 20),
+        compiler_params=pltpu.CompilerParams(vmem_limit_bytes=62_000_000),
         name="degree",
     )(block_count, features.T, adjacency)
     gathered = lax.all_gather(sent, "col", axis=0, tiled=False)
@@ -141,32 +151,38 @@
         name="transform",
     )(gathered, weight.T)
 
-    def shift(step):
-        return lax.ppermute(z, "row", [(s, (s + step) % devices) for s in range(devices)])
-
-    pair, before, after = shift(devices // 2), shift(1), shift(-1)
-    near, base, offset = pl.pallas_call(
-        lambda *refs: blocks_kernel(nblk, *refs),
+    def exchange(values, targets):
+        return lax.ppermute(values, "row", [(s, targets(s)) for s in range(devices) if targets(s) is not None])
+
+    half = devices // 2
+    line = LINE
+    opposite_first = exchange(z, lambda s: (s + half) % devices if s % line < line // 2 else None)
+    before = exchange(z, lambda s: s + 1 if s + 1 < devices else None)
+    after = exchange(z, lambda s: s - 1 if s > 0 else None)
+    near, base, offset, same = pl.pallas_call(
+        blocks_kernel,
         out_shape=(
             jax.ShapeDtypeStruct((3, nodes, 2 * bsize), BF16),
             jax.ShapeDtypeStruct((outs, nodes), F32),
             jax.ShapeDtypeStruct((outs, 1), F32),
+            jax.ShapeDtypeStruct((outs, nodes), BF16),
         ),
         in_specs=[smem, smem, vmem, vmem, vmem],
-        out_specs=(vmem, vmem, vmem),
+        out_specs=(vmem, vmem, vmem, vmem),
         scratch_shapes=[pltpu.VMEM((8, nodes, bsize), F32)],
         cost_estimate=pl.CostEstimate(flops=70_000_000, bytes_accessed=2_500_000, transcendentals=0),
         compiler_params=pltpu.CompilerParams(vmem_limit_bytes=12 << 20),
         name="blocks",
     )(block_count, block_cols, adjacency, z, bias.reshape(1, -1))
+    opposite_last = exchange(same, lambda s: None if s % line < line // 2 else (s + half) % devices)
     out = pl.pallas_call(
         finish_kernel,
         out_shape=jax.ShapeDtypeStruct((outs, nodes), BF16),
-        in_specs=[vmem] * 7,
+        in_specs=[vmem] * 8,
         out_specs=vmem,
         compiler_params=pltpu.CompilerParams(vmem_limit_bytes=4 << 20),
         name="finish",
-    )(before, after, pair, near, base, scale, offset)
+    )(after, before, opposite_first, opposite_last, near, base, scale, offset)
     return out.T
 
 

time: 47.5 us -> 34 us (0.72)
  the two profiles are of different devices: /device:TPU:8 before, /device:TPU:32 now
where the time goes in v2:
time: 34 us; the launch traced here: 33.8 us
  starting transfers between devices  23.9 us (70%)
  blocking collectives  5.73 us (17%)
  Pallas kernels  4 us (12%)
    ppermute x4, starting transfers between devices, exchange(): lax.ppermute(values, 'row', [(s, targets(s)) for s in range(devices) if t...  23.9 us
    all_gather x1, blocking collectives, on_device(): gathered = lax.all_gather(sent, 'col', axis=0, tiled=False)  5.73 us
    pallas_call x1, Pallas kernels, on_device(): pl.pallas_call(degree_kernel, out_shape=jax.ShapeDtypeStruct((width + 16,...  2.07 us
    pallas_call x1, Pallas kernels, on_device(): pl.pallas_call(blocks_kernel, out_shape=(jax.ShapeDtypeStruct((3, nodes,...  0.9 us
    pallas_call x1, Pallas kernels, on_device(): pl.pallas_call(finish_kernel, out_shape=jax.ShapeDtypeStruct((outs, nodes...  0.89 us
  transfers between devices with their start and end apart: 4, of which 0 were waited for; matrix products, arithmetic and copies ran while one was open for 0% of the time, Pallas kernels for 3%

profile of v2, /device:TPU:32, one launch (start us, length us, event | category | flops | bytes accessed | tf_op | source)
XLA Modules:
  0.0 33.8 jit_solution(1362243842157996)
XLA Ops:
  0.0 0.0 copy-start.2
  0.0 0.0 copy-start
  0.0 0.0 copy-start.1
  0.0 0.0 copy-start.3
  0.0 0.0 copy-start.4
  0.0 2.1 %degree.1 = bf16[80,256]{1,0:T(8,128)(2,1)} custom-call(s32[2]{0:T(128)} %count_ref.1, bf16[64,256]{1,0:T(8,128)(2,1)} %bitcast.8, bf16[2,32,128,128]{3,2,1,0:T(8,128)(2,1)} %tiles.1), custom_call_target="tpu_custom_call" | custom-call | tf_op jit(solution)/shard_map/degree/pallas_call | solution.py:127
  2.1 5.7 %all-gather = bf16[320,256]{1,0:T(8,128)(2,1)S(1)} all-gather(bf16[80,256]{1,0:T(8,128)(2,1)} %degree.1), channel_id=2, replica_groups=mesh['row'=192,'col'=4] {'col'}, dimensions={0}, use_global_device_ids=true | all-gather | bytes 204800 | tf_op jit(solution)/shard_map/all_gather | solution.py:141
  7.8 0.0 copy-done.1
  7.8 0.1 transform.1
  8.0 11.0 %collective-permute-start.2 = (bf16[64,256]{1,0:T(8,128)(2,1)S(1)}, bf16[64,256]{1,0:T(8,128)(2,1)S(1)}, u32[]{:S(2)}, u32[]{:S(2)}) collective-permute-start(bf16[64,256]{1,0:T(8,128)(2,1)S(1)} %get-tuple-element.11.z_ref), channel_id=1, source_target_pairs={{0,384},{4,388},{8,392},{12,396},{16,400},{20,404},{48,432},{52,43... | collective-permute-start | bytes 98312 | tf_op jit(solution)/shard_map/ppermute | solution.py:155
  19.0 1.9 %collective-permute-start.1 = (bf16[64,256]{1,0:T(8,128)(2,1)S(1)}, bf16[64,256]{1,0:T(8,128)(2,1)S(1)}, u32[]{:S(2)}, u32[]{:S(2)}) collective-permute-start(bf16[64,256]{1,0:T(8,128)(2,1)S(1)} %get-tuple-element.11.z_ref), channel_id=1, source_target_pairs={{0,4},{4,8},{8,12},{12,16},{16,20},{20,24},{24,28},{28,32},{32,36}... | collective-permute-start | bytes 98312 | tf_op jit(solution)/shard_map/ppermute | solution.py:155
  20.9 10.3 %collective-permute-start = (bf16[64,256]{1,0:T(8,128)(2,1)S(1)}, bf16[64,256]{1,0:T(8,128)(2,1)S(1)}, u32[]{:S(2)}, u32[]{:S(2)}) collective-permute-start(bf16[64,256]{1,0:T(8,128)(2,1)S(1)} %get-tuple-element.11.z_ref), channel_id=1, source_target_pairs={{4,0},{8,4},{12,8},{16,12},{20,16},{24,20},{28,24},{32,28},{36,32}... | collective-permute-start | bytes 98312 | tf_op jit(solution)/shard_map/ppermute | solution.py:155
  31.2 0.0 copy-done.2
  31.2 0.0 copy-done
  31.2 0.0 copy-done.3
  31.2 0.0 copy-done.4
  31.2 0.9 %blocks.1 = (bf16[3,256,256]{2,1,0:T(8,128)(2,1)S(1)}, f32[64,256]{1,0:T(8,128)S(1)}, f32[64,1]{1,0:T(8,128)S(1)}, bf16[64,256]{1,0:T(8,128)(2,1)S(1)}) custom-call(s32[2]{0:T(128)S(1)} %copy-done.2, s32[2,32]{1,0:T(2,128)S(1)} %copy-done.3, bf16[2,32,128,128]{3,2,1,0:T(8,128)(2,1)S(1)} %copy-done, bf16[64,256]{1,0:T(8,128)(2,1)S(1)} %get-tuple-element.11.z_ref, ...), custom_call_target="tpu_custom_call" | custom-call | flops 70000000 | bytes 2500000 | tf_op jit(solution)/shard_map/blocks/pallas_call | solution.py:162
  32.1 0.7 %collective-permute-start.3 = (bf16[64,256]{1,0:T(8,128)(2,1)S(1)}, bf16[64,256]{1,0:T(8,128)(2,1)S(1)}, u32[]{:S(2)}, u32[]{:S(2)}) collective-permute-start(bf16[64,256]{1,0:T(8,128)(2,1)S(1)} %get-tuple-element.12), channel_id=1, source_target_pairs={{24,408},{28,412},{32,416},{36,420},{40,424},{44,428},{72,456},{76... | collective-permute-start | bytes 98312 | tf_op jit(solution)/shard_map/ppermute | solution.py:155
  32.8 0.0 collective-permute-done.2.first_ref
  32.8 0.0 collective-permute-done.1.before_ref
  32.8 0.0 collective-permute-done.after_ref
  32.9 0.0 collective-permute-done.3.last_ref
  32.9 0.9 %finish.1 = bf16[64,256]{1,0:T(8,128)(2,1)} custom-call(bf16[64,256]{1,0:T(8,128)(2,1)S(1)} %collective-permute-done.after_ref, bf16[64,256]{1,0:T(8,128)(2,1)S(1)} %collective-permute-done.1.before_ref, bf16[64,256]{1,0:T(8,128)(2,1)S(1)} %collective-permute-done.2.first_ref, bf16[64,256]{1,0:T(8,128)(2,1)S(1)} %collective-permute-done.3.last_ref, ...), custom_call_target="tpu_custom_call" | custom-call | tf_op jit(solution)/shard_map/finish/pallas_call | solution.py:178
Async XLA Ops:
  0.0 31.2 %copy-start.2 = (s32[2]{0:T(128)S(1)}, s32[2]{0:T(128)}, u32[]{:S(2)}) copy-start(s32[2]{0:T(128)} %count_ref.1) | copy-start | bytes 28
  0.0 31.2 %copy-start = (bf16[2,32,128,128]{3,2,1,0:T(8,128)(2,1)S(1)}, bf16[2,32,128,128]{3,2,1,0:T(8,128)(2,1)}, u32[]{:S(2)}) copy-start(bf16[2,32,128,128]{3,2,1,0:T(8,128)(2,1)} %tiles.1) | copy-start | bytes 6291460
  0.0 7.8 %copy-start.1 = (bf16[256,64]{0,1:T(8,128)(2,1)S(1)}, bf16[256,64]{0,1:T(8,128)(2,1)}, u32[]{:S(2)}) copy-start(bf16[256,64]{0,1:T(8,128)(2,1)} %param.7) | copy-start | bytes 98308
  0.0 31.2 %copy-start.3 = (s32[2,32]{1,0:T(2,128)S(1)}, s32[2,32]{1,0:T(2,128)}, u32[]{:S(2)}) copy-start(s32[2,32]{1,0:T(2,128)} %cols_ref.1) | copy-start | bytes 772
  0.0 31.2 %copy-start.4 = (f32[64]{0:T(128)S(1)}, f32[64]{0:T(128)}, u32[]{:S(2)}) copy-start(f32[64]{0:T(128)} %param.8) | copy-start | bytes 772
  8.0 24.8 %collective-permute-start.2 = (bf16[64,256]{1,0:T(8,128)(2,1)S(1)}, bf16[64,256]{1,0:T(8,128)(2,1)S(1)}, u32[]{:S(2)}, u32[]{:S(2)}) collective-permute-start(bf16[64,256]{1,0:T(8,128)(2,1)S(1)} %get-tuple-element.11.z_ref), channel_id=1, source_target_pairs={{0,384},{4,388},{8,392},{12,396},{16,400},{20,404},{48,432},{52,43... | collective-permute-start | bytes 98312 | tf_op jit(solution)/shard_map/ppermute | solution.py:155
  19.0 13.8 %collective-permute-start.1 = (bf16[64,256]{1,0:T(8,128)(2,1)S(1)}, bf16[64,256]{1,0:T(8,128)(2,1)S(1)}, u32[]{:S(2)}, u32[]{:S(2)}) collective-permute-start(bf16[64,256]{1,0:T(8,128)(2,1)S(1)} %get-tuple-element.11.z_ref), channel_id=1, source_target_pairs={{0,4},{4,8},{8,12},{12,16},{16,20},{20,24},{24,28},{28,32},{32,36}... | collective-permute-start | bytes 98312 | tf_op jit(solution)/shard_map/ppermute | solution.py:155
  20.9 11.9 %collective-permute-start = (bf16[64,256]{1,0:T(8,128)(2,1)S(1)}, bf16[64,256]{1,0:T(8,128)(2,1)S(1)}, u32[]{:S(2)}, u32[]{:S(2)}) collective-permute-start(bf16[64,256]{1,0:T(8,128)(2,1)S(1)} %get-tuple-element.11.z_ref), channel_id=1, source_target_pairs={{4,0},{8,4},{12,8},{16,12},{20,16},{24,20},{28,24},{32,28},{36,32}... | collective-permute-start | bytes 98312 | tf_op jit(solution)/shard_map/ppermute | solution.py:155
  32.1 0.7 %collective-permute-start.3 = (bf16[64,256]{1,0:T(8,128)(2,1)S(1)}, bf16[64,256]{1,0:T(8,128)(2,1)S(1)}, u32[]{:S(2)}, u32[]{:S(2)}) collective-permute-start(bf16[64,256]{1,0:T(8,128)(2,1)S(1)} %get-tuple-element.12), channel_id=1, source_target_pairs={{24,408},{28,412},{32,416},{36,420},{40,424},{44,428},{72,456},{76... | collective-permute-start | bytes 98312 | tf_op jit(solution)/shard_map/ppermute | solution.py:155

commit v3 on v0

v3 whole, which is shorter than its diff:
```python
import jax
import jax.numpy as jnp
from jax import lax
from jax.experimental import pallas as pl
from jax.experimental.pallas import tpu as pltpu
from jax.sharding import PartitionSpec as P

F32 = jnp.float32
BF16 = jnp.bfloat16
SMEM = pltpu.MemorySpace.SMEM
VMEM = pltpu.MemorySpace.VMEM
NT = (((1,), (1,)), ((), ()))
LINE = 12
NEAR = 6


def split(value):
    high = value.astype(BF16)
    return high, (value - high.astype(F32)).astype(BF16)


def clear_kernel(out_ref):
    out_ref[...] = jnp.zeros_like(out_ref)


def transform_kernel(
    count_ref, cols_ref, tiles, full_ref, weight_ref, bias_ref, _, z_ref, blocks_ref, scale_ref, offset_ref
):
    own_rows, _, bsize, _ = tiles.shape
    first = lax.axis_index("row") * own_rows - 2
    for r in range(own_rows):
        rows = slice(r * bsize, (r + 1) * bsize)
        blocks_ref[6 + r, rows, :] = tiles[r, 1]

        def step(k, _):
            place = jnp.clip(cols_ref[r, k] - first, 0, 5)
            blocks_ref[place, rows, :] += tiles[r, k]
            return 0

        step(0, 0)
        lax.fori_loop(2, count_ref[r], step, 0)
    total = blocks_ref[0].astype(F32)
    for b in range(1, blocks_ref.shape[0]):
        total += blocks_ref[b].astype(F32)
    ones = jnp.ones((16, bsize), BF16)
    high, low = split(total)
    degree = 1.0 + (
        lax.dot_general(ones, high, NT, preferred_element_type=F32)
        + lax.dot_general(ones, low, NT, preferred_element_type=F32)
    )
    scale = lax.rsqrt(degree[:1, :])
    product = jnp.dot(weight_ref[...], full_ref[...], preferred_element_type=F32)
    z_ref[...] = (product * scale).astype(BF16)
    scale_ref[...] = jnp.broadcast_to(scale, scale_ref.shape)
    outs = bias_ref.shape[1]
    eye = lax.broadcasted_iota(jnp.int32, (outs, outs), 0) == lax.broadcasted_iota(jnp.int32, (outs, outs), 1)
    offset_ref[...] = jnp.sum(jnp.where(eye, bias_ref[...], 0.0), axis=1, keepdims=True)


def finish_kernel(
    last_ref, after_ref, first_ref, before_ref, z_ref, blocks_ref, scale_ref, offset_ref, out_ref
):
    own = z_ref[...]
    total = own.astype(F32)
    before = before_ref[...]
    after = after_ref[...]
    pair = first_ref[...] + last_ref[...]
    for slot, z in enumerate((before, own, after, pair)):
        block = jnp.concatenate([blocks_ref[2 * slot], blocks_ref[2 * slot + 1]], axis=1)
        total += lax.dot_general(z, block, NT, preferred_element_type=F32)
    result = scale_ref[:1, :] * total + offset_ref[...]
    out_ref[...] = jnp.maximum(result, 0.0).astype(BF16)


def on_device(features, weight, bias, adjacency, block_cols, block_count):
    own_rows, _, bsize, _ = adjacency.shape
    devices = lax.axis_size("row")
    nodes = features.shape[0]
    outs = weight.shape[1]
    vmem = pl.BlockSpec(memory_space=VMEM)
    smem = pl.BlockSpec(memory_space=SMEM)

    cleared = pl.pallas_call(
        clear_kernel,
        out_shape=jax.ShapeDtypeStruct((8, nodes, bsize), BF16),
        out_specs=vmem,
        compiler_params=pltpu.CompilerParams(vmem_limit_bytes=4 << 20),
        cost_estimate=pl.CostEstimate(flops=1 << 32, bytes_accessed=64 << 20, transcendentals=0),
        name="clear",
    )()
    panel, cleared = lax.optimization_barrier((features.T, cleared))
    full = lax.all_gather(panel, "col", axis=0, tiled=True)
    z, blocks, scale, offset = pl.pallas_call(
        transform_kernel,
        out_shape=(
            jax.ShapeDtypeStruct((outs, nodes), BF16),
            jax.ShapeDtypeStruct((8, nodes, bsize), BF16),
            jax.ShapeDtypeStruct((8, nodes), F32),
            jax.ShapeDtypeStruct((outs, 1), F32),
        ),
        in_specs=[smem, smem, vmem, vmem, vmem, vmem, vmem],
        input_output_aliases={6: 1},
        out_specs=(vmem,) * 4,
        compiler_params=pltpu.CompilerParams(vmem_limit_bytes=12 << 20),
        name="transform",
    )(block_count, block_cols, adjacency, full, weight.T, bias.reshape(1, -1), cleared)

    def exchange(targets):
        return lax.ppermute(z, "row", [(s, targets(s)) for s in range(devices) if targets(s) is not None])

    half = devices // 2

    def plus(s):
        return s + 1 if s + 1 < devices else None

    def minus(s):
        return s - 1 if s > 0 else None

    def pair(s):
        return (s + half) % devices

    before = exchange(plus)
    first = exchange(lambda s: pair(s) if s % LINE < NEAR or (s >= half and s % LINE < LINE - 1) else None)
    after = exchange(minus)
    last = exchange(lambda s: pair(s) if s % LINE == LINE - 1 or (s < half and s % LINE >= NEAR) else None)
    out = pl.pallas_call(
        finish_kernel,
        out_shape=jax.ShapeDtypeStruct((outs, nodes), BF16),
        in_specs=[vmem] * 8,
        out_specs=vmem,
        compiler_params=pltpu.CompilerParams(vmem_limit_bytes=4 << 20),
        name="finish",
    )(last, after, first, before, z, blocks, scale, offset)
    return out.T


def solution(mesh):
    return jax.shard_map(
        on_device,
        mesh=mesh,
        in_specs=(
            P("row", "col"),
            P(None, "col"),
            P("col"),
            P("row", None, None, None),
            P("row", None),
            P("row"),
        ),
        out_specs=P("row", "col"),
        check_vma=False,
    )
```

time: 229 us -> 30.7 us (0.13)
  waiting for transfers between devices: 192 us -> 0.89 us
  starting transfers between devices: 0.01 us -> 21.2 us
  between operations: 13.5 us -> 0.11 us
  local copies, waits for them, and re-layouts: 11 us -> 0.66 us
  other arithmetic: 3.67 us -> 0 us
    all_gather x1 -> x0, waiting for transfers between devices: 192 us -> none  [on_device(): gathered = lax.all_gather(own_panel, 'row', axis=0, tiled=True)]
    ppermute x0 -> x4, starting transfers between devices: none -> 21.2 us  [exchange(): lax.ppermute(z, 'row', [(s, targets(s)) for s in range(devices) if target...]
    reshape x1 -> x0, local copies, waits for them, and re-layouts: 7.23 us -> none  [aggregate(): gathered.reshape(gathered.shape[0] // bsize, bsize, gathered.shape[1])]
    gather x1 -> x0, local copies, waits for them, and re-layouts: 3.68 us -> none  [aggregate(): picked = blocks[cols]]
  transfers between devices with their start and end apart: 1 -> 4, of which waited for: 1 -> 1; matrix products, arithmetic and copies ran while one was open for 0% -> 0% of each run, Pallas kernels for 0% -> 0%
where the time goes in v3:
time: 30.7 us; the launch traced here: 30.5 us
  starting transfers between devices  21.2 us (69%)
  blocking collectives  5.41 us (18%)
  Pallas kernels  2.28 us (7%)
  waiting for transfers between devices  0.89 us (3%)
  local copies, waits for them, and re-layouts  0.66 us (2%)
    ppermute x4, starting transfers between devices, exchange(): lax.ppermute(z, 'row', [(s, targets(s)) for s in range(devices) if target...  21.2 us
    all_gather x1, blocking collectives, on_device(): full = lax.all_gather(panel, 'col', axis=0, tiled=True)  5.41 us
    pallas_call x1, Pallas kernels, on_device(): pl.pallas_call(transform_kernel, out_shape=(jax.ShapeDtypeStruct((outs, n...  1.3 us
    pallas_call x1, Pallas kernels, on_device(): pl.pallas_call(finish_kernel, out_shape=jax.ShapeDtypeStruct((outs, nodes...  0.91 us
    ppermute x4, waiting for transfers between devices, exchange(): lax.ppermute(z, 'row', [(s, targets(s)) for s in range(devices) if target...  0.89 us
    unnamed x12, local copies, waits for them, and re-layouts  0.66 us
  transfers between devices with their start and end apart: 4, of which 1 were waited for; matrix products, arithmetic and copies ran while one was open for 0% of the time, Pallas kernels for 0%

profile of v3, /device:TPU:56, one launch (start us, length us, event | category | flops | bytes accessed | tf_op | source)
XLA Modules:
  0.0 30.5 jit_solution(11660177767338405803)
XLA Ops:
  0.0 0.0 copy-start.5
  0.0 0.0 copy-start.3
  0.0 0.0 copy-start.2
  0.0 0.0 copy-start
  0.0 0.0 copy-start.4
  0.0 0.0 copy-start.1
  0.0 0.1 clear.1._
  0.1 0.6 %copy-done.5 = bf16[256,64]{0,1:T(8,128)(2,1)S(1)} copy-done((bf16[256,64]{0,1:T(8,128)(2,1)S(1)}, bf16[256,64]{0,1:T(8,128)(2,1)}, u32[]{:S(2)}) %copy-start.5) | copy-done | bytes 32792
  0.8 5.4 %all_gather.3.full_ref = bf16[256,256]{1,0:T(8,128)(2,1)S(1)} all-gather(bf16[64,256]{1,0:T(8,128)(2,1)S(1)} %bitcast.6), channel_id=1, replica_groups=mesh['row'=192,'col'=4] {'col'}, dimensions={0}, use_global_device_ids=true | all-gather | bytes 163840 | tf_op jit(solution)/shard_map/all_gather | solution.py:92
  6.2 0.0 copy-done.3
  6.2 0.0 copy-done.2
  6.2 0.0 copy-done
  6.2 0.0 copy-done.4
  6.2 0.0 copy-done.1
  6.2 1.3 %transform.1 = (bf16[64,256]{1,0:T(8,128)(2,1)S(1)}, bf16[8,256,128]{2,1,0:T(8,128)(2,1)S(1)}, f32[8,256]{1,0:T(8,128)S(1)}, f32[64,1]{1,0:T(8,128)S(1)}) custom-call(s32[2]{0:T(128)S(1)} %copy-done.3, s32[2,32]{1,0:T(2,128)S(1)} %copy-done.2, bf16[2,32,128,128]{3,2,1,0:T(8,128)(2,1)S(1)} %copy-done, ...), custom_call_target="tpu_custom_call", output_to_operand_aliasing={{1}: (6, {})} | custom-call | tf_op jit(solution)/shard_map/transform/pallas_call | solution.py:93
  7.5 4.2 %collective-permute-start.3 = (bf16[64,256]{1,0:T(8,128)(2,1)S(1)}, bf16[64,256]{1,0:T(8,128)(2,1)S(1)}, u32[]{:S(2)}, u32[]{:S(2)}) collective-permute-start(bf16[64,256]{1,0:T(8,128)(2,1)S(1)} %get-tuple-element.13.z_ref), channel_id=1, source_target_pairs={{0,4},{4,8},{8,12},{12,16},{16,20},{20,24},{24,28},{28,32},{32,36}... | collective-permute-start | bytes 98312 | tf_op jit(solution)/shard_map/ppermute | solution.py:109
  11.7 4.4 %collective-permute-start.2 = (bf16[64,256]{1,0:T(8,128)(2,1)S(1)}, bf16[64,256]{1,0:T(8,128)(2,1)S(1)}, u32[]{:S(2)}, u32[]{:S(2)}) collective-permute-start(bf16[64,256]{1,0:T(8,128)(2,1)S(1)} %get-tuple-element.13.z_ref), channel_id=1, source_target_pairs={{0,384},{4,388},{8,392},{12,396},{16,400},{20,404},{48,432},{52,43... | collective-permute-start | bytes 98312 | tf_op jit(solution)/shard_map/ppermute | solution.py:109
  16.2 11.9 %collective-permute-start.1 = (bf16[64,256]{1,0:T(8,128)(2,1)S(1)}, bf16[64,256]{1,0:T(8,128)(2,1)S(1)}, u32[]{:S(2)}, u32[]{:S(2)}) collective-permute-start(bf16[64,256]{1,0:T(8,128)(2,1)S(1)} %get-tuple-element.13.z_ref), channel_id=1, source_target_pairs={{4,0},{8,4},{12,8},{16,12},{20,16},{24,20},{28,24},{32,28},{36,32}... | collective-permute-start | bytes 98312 | tf_op jit(solution)/shard_map/ppermute | solution.py:109
  28.1 0.7 %collective-permute-start = (bf16[64,256]{1,0:T(8,128)(2,1)S(1)}, bf16[64,256]{1,0:T(8,128)(2,1)S(1)}, u32[]{:S(2)}, u32[]{:S(2)}) collective-permute-start(bf16[64,256]{1,0:T(8,128)(2,1)S(1)} %get-tuple-element.13.z_ref), channel_id=1, source_target_pairs={{24,408},{28,412},{32,416},{36,420},{40,424},{44,428},{72,456},{76... | collective-permute-start | bytes 98312 | tf_op jit(solution)/shard_map/ppermute | solution.py:109
  28.7 0.0 collective-permute-done.3.before_ref
  28.7 0.0 collective-permute-done.2.first_ref
  28.7 0.9 %collective-permute-done.1.after_ref = bf16[64,256]{1,0:T(8,128)(2,1)S(1)} collective-permute-done((bf16[64,256]{1,0:T(8,128)(2,1)S(1)}, bf16[64,256]{1,0:T(8,128)(2,1)S(1)}, u32[]{:S(2)}, u32[]{:S(2)}) %collective-permute-start.1) | collective-permute-done | bytes 32800 | tf_op jit(solution)/shard_map/ppermute | solution.py:109
  29.6 0.0 collective-permute-done.last_ref
  29.6 0.9 %finish.1 = bf16[64,256]{1,0:T(8,128)(2,1)} custom-call(bf16[64,256]{1,0:T(8,128)(2,1)S(1)} %collective-permute-done.last_ref, bf16[64,256]{1,0:T(8,128)(2,1)S(1)} %collective-permute-done.1.after_ref, bf16[64,256]{1,0:T(8,128)(2,1)S(1)} %collective-permute-done.2.first_ref, bf16[64,256]{1,0:T(8,128)(2,1)S(1)} %collective-permute-done.3.before_ref, ...), custom_call_target="tpu_custom_call" | custom-call | tf_op jit(solution)/shard_map/finish/pallas_call | solution.py:126
Async XLA Ops:
  0.0 0.8 %copy-start.5 = (bf16[256,64]{0,1:T(8,128)(2,1)S(1)}, bf16[256,64]{0,1:T(8,128)(2,1)}, u32[]{:S(2)}) copy-start(bf16[256,64]{0,1:T(8,128)(2,1)} %param.6) | copy-start | bytes 98308
  0.0 6.2 %copy-start.3 = (s32[2]{0:T(128)S(1)}, s32[2]{0:T(128)}, u32[]{:S(2)}) copy-start(s32[2]{0:T(128)} %count_ref.1) | copy-start | bytes 28
  0.0 6.2 %copy-start.2 = (s32[2,32]{1,0:T(2,128)S(1)}, s32[2,32]{1,0:T(2,128)}, u32[]{:S(2)}) copy-start(s32[2,32]{1,0:T(2,128)} %cols_ref.1) | copy-start | bytes 772
  0.0 6.2 %copy-start = (bf16[2,32,128,128]{3,2,1,0:T(8,128)(2,1)S(1)}, bf16[2,32,128,128]{3,2,1,0:T(8,128)(2,1)}, u32[]{:S(2)}) copy-start(bf16[2,32,128,128]{3,2,1,0:T(8,128)(2,1)} %tiles.1) | copy-start | bytes 6291460
  0.0 6.2 %copy-start.4 = (f32[64]{0:T(128)S(1)}, f32[64]{0:T(128)}, u32[]{:S(2)}) copy-start(f32[64]{0:T(128)} %param.8) | copy-start | bytes 772
  0.0 6.2 %copy-start.1 = (bf16[256,64]{0,1:T(8,128)(2,1)S(1)}, bf16[256,64]{0,1:T(8,128)(2,1)}, u32[]{:S(2)}) copy-start(bf16[256,64]{0,1:T(8,128)(2,1)} %param.7) | copy-start | bytes 98308
  7.5 21.2 %collective-permute-start.3 = (bf16[64,256]{1,0:T(8,128)(2,1)S(1)}, bf16[64,256]{1,0:T(8,128)(2,1)S(1)}, u32[]{:S(2)}, u32[]{:S(2)}) collective-permute-start(bf16[64,256]{1,0:T(8,128)(2,1)S(1)} %get-tuple-element.13.z_ref), channel_id=1, source_target_pairs={{0,4},{4,8},{8,12},{12,16},{16,20},{20,24},{24,28},{28,32},{32,36}... | collective-permute-start | bytes 98312 | tf_op jit(solution)/shard_map/ppermute | solution.py:109
  11.7 17.0 %collective-permute-start.2 = (bf16[64,256]{1,0:T(8,128)(2,1)S(1)}, bf16[64,256]{1,0:T(8,128)(2,1)S(1)}, u32[]{:S(2)}, u32[]{:S(2)}) collective-permute-start(bf16[64,256]{1,0:T(8,128)(2,1)S(1)} %get-tuple-element.13.z_ref), channel_id=1, source_target_pairs={{0,384},{4,388},{8,392},{12,396},{16,400},{20,404},{48,432},{52,43... | collective-permute-start | bytes 98312 | tf_op jit(solution)/shard_map/ppermute | solution.py:109
  16.2 13.4 %collective-permute-start.1 = (bf16[64,256]{1,0:T(8,128)(2,1)S(1)}, bf16[64,256]{1,0:T(8,128)(2,1)S(1)}, u32[]{:S(2)}, u32[]{:S(2)}) collective-permute-start(bf16[64,256]{1,0:T(8,128)(2,1)S(1)} %get-tuple-element.13.z_ref), channel_id=1, source_target_pairs={{4,0},{8,4},{12,8},{16,12},{20,16},{24,20},{28,24},{32,28},{36,32}... | collective-permute-start | bytes 98312 | tf_op jit(solution)/shard_map/ppermute | solution.py:109
  28.1 1.6 %collective-permute-start = (bf16[64,256]{1,0:T(8,128)(2,1)S(1)}, bf16[64,256]{1,0:T(8,128)(2,1)S(1)}, u32[]{:S(2)}, u32[]{:S(2)}) collective-permute-start(bf16[64,256]{1,0:T(8,128)(2,1)S(1)} %get-tuple-element.13.z_ref), channel_id=1, source_target_pairs={{24,408},{28,412},{32,416},{36,420},{40,424},{44,428},{72,456},{76... | collective-permute-start | bytes 98312 | tf_op jit(solution)/shard_map/ppermute | solution.py:109

commit v4 on v3

--- a/solution.py
+++ b/solution.py
@@ -12,6 +12,7 @@
 NT = (((1,), (1,)), ((), ()))
 LINE = 12
 NEAR = 6
+UNROLL = 3
 
 
 def split(value):
@@ -19,29 +20,43 @@
     return high, (value - high.astype(F32)).astype(BF16)
 
 
-def clear_kernel(out_ref):
-    out_ref[...] = jnp.zeros_like(out_ref)
+def clear_kernel(*out_refs):
+    for ref in out_refs:
+        ref[...] = jnp.zeros_like(ref)
 
 
 def transform_kernel(
-    count_ref, cols_ref, tiles, full_ref, weight_ref, bias_ref, _, z_ref, blocks_ref, scale_ref, offset_ref
+    count_ref, cols_ref, tiles, full_ref, weight_ref, bias_ref, _a, _b, z_ref, *refs
 ):
+    *blocks, scale_ref, offset_ref = refs
     own_rows, _, bsize, _ = tiles.shape
     first = lax.axis_index("row") * own_rows - 2
+    spare = blocks[0].shape[0] - 1
+    counts = [count_ref[r] for r in range(own_rows)]
+
+    def add(r, k):
+        place = jnp.where(k < counts[r], jnp.clip(cols_ref[r, k] - first, 0, 5), spare)
+        blocks[r][place] += tiles[r, k]
+
     for r in range(own_rows):
-        rows = slice(r * bsize, (r + 1) * bsize)
-        blocks_ref[6 + r, rows, :] = tiles[r, 1]
+        blocks[r][6 + r] = tiles[r, 1]
+        add(r, 0)
 
-        def step(k, _):
-            place = jnp.clip(cols_ref[r, k] - first, 0, 5)
-            blocks_ref[place, rows, :] += tiles[r, k]
-            return 0
+    def step(k, _):
+        for u in range(UNROLL):
+            for r in range(own_rows):
+                add(r, 2 + k * UNROLL + u)
+        return 0
 
-        step(0, 0)
-        lax.fori_loop(2, count_ref[r], step, 0)
-    total = blocks_ref[0].astype(F32)
-    for b in range(1, blocks_ref.shape[0]):
-        total += blocks_ref[b].astype(F32)
+    longest = jnp.maximum(counts[0], counts[1])
+    lax.fori_loop(0, (longest - 2 + UNROLL - 1) // UNROLL, step, 0)
+    sums = []
+    for r in range(own_rows):
+        total = blocks[r][0].astype(F32)
+        for b in range(1, spare):
+            total += blocks[r][b].astype(F32)
+        sums.append(total)
+    total = jnp.concatenate(sums, axis=0)
     ones = jnp.ones((16, bsize), BF16)
     high, low = split(total)
     degree = 1.0 + (
@@ -58,7 +73,7 @@
 
 
 def finish_kernel(
-    last_ref, after_ref, first_ref, before_ref, z_ref, blocks_ref, scale_ref, offset_ref, out_ref
+    last_ref, after_ref, first_ref, before_ref, z_ref, upper_ref, lower_ref, scale_ref, offset_ref, out_ref
 ):
     own = z_ref[...]
     total = own.astype(F32)
@@ -66,7 +81,8 @@
     after = after_ref[...]
     pair = first_ref[...] + last_ref[...]
     for slot, z in enumerate((before, own, after, pair)):
-        block = jnp.concatenate([blocks_ref[2 * slot], blocks_ref[2 * slot + 1]], axis=1)
+        rows = [jnp.concatenate([ref[2 * slot], ref[2 * slot + 1]], axis=1) for ref in (upper_ref, lower_ref)]
+        block = jnp.concatenate(rows, axis=0)
         total += lax.dot_general(z, block, NT, preferred_element_type=F32)
     result = scale_ref[:1, :] * total + offset_ref[...]
     out_ref[...] = jnp.maximum(result, 0.0).astype(BF16)
@@ -80,30 +96,32 @@
     vmem = pl.BlockSpec(memory_space=VMEM)
     smem = pl.BlockSpec(memory_space=SMEM)
 
+    sums = jax.ShapeDtypeStruct((9, bsize, bsize), BF16)
     cleared = pl.pallas_call(
         clear_kernel,
-        out_shape=jax.ShapeDtypeStruct((8, nodes, bsize), BF16),
-        out_specs=vmem,
+        out_shape=(sums,) * own_rows,
+        out_specs=(vmem,) * own_rows,
         compiler_params=pltpu.CompilerParams(vmem_limit_bytes=4 << 20),
-        cost_estimate=pl.CostEstimate(flops=1 << 32, bytes_accessed=64 << 20, transcendentals=0),
+        cost_estimate=pl.CostEstimate(flops=550_000_000, bytes_accessed=1 << 20, transcendentals=0),
         name="clear",
     )()
     panel, cleared = lax.optimization_barrier((features.T, cleared))
     full = lax.all_gather(panel, "col", axis=0, tiled=True)
-    z, blocks, scale, offset = pl.pallas_call(
+    z, upper, lower, scale, offset = pl.pallas_call(
         transform_kernel,
         out_shape=(
             jax.ShapeDtypeStruct((outs, nodes), BF16),
-            jax.ShapeDtypeStruct((8, nodes, bsize), BF16),
+            sums,
+            sums,
             jax.ShapeDtypeStruct((8, nodes), F32),
             jax.ShapeDtypeStruct((outs, 1), F32),
         ),
-        in_specs=[smem, smem, vmem, vmem, vmem, vmem, vmem],
-        input_output_aliases={6: 1},
-        out_specs=(vmem,) * 4,
+        in_specs=[smem, smem] + [vmem] * 6,
+        input_output_aliases={6: 1, 7: 2},
+        out_specs=(vmem,) * 5,
         compiler_params=pltpu.CompilerParams(vmem_limit_bytes=12 << 20),
         name="transform",
-    )(block_count, block_cols, adjacency, full, weight.T, bias.reshape(1, -1), cleared)
+    )(block_count, block_cols, adjacency, full, weight.T, bias.reshape(1, -1), *cleared)
 
     def exchange(targets):
         return lax.ppermute(z, "row", [(s, targets(s)) for s in range(devices) if targets(s) is not None])
@@ -126,11 +144,11 @@
     out = pl.pallas_call(
         finish_kernel,
         out_shape=jax.ShapeDtypeStruct((outs, nodes), BF16),
-        in_specs=[vmem] * 8,
+        in_specs=[vmem] * 9,
         out_specs=vmem,
         compiler_params=pltpu.CompilerParams(vmem_limit_bytes=4 << 20),
         name="finish",
-    )(last, after, first, before, z, blocks, scale, offset)
+    )(last, after, first, before, z, upper, lower, scale, offset)
     return out.T
 
 

time: 30.7 us -> 30.9 us (level)
  local copies, waits for them, and re-layouts: 0.66 us -> 0.02 us
  starting transfers between devices: 21.2 us -> 21.6 us
  blocking collectives: 5.41 us -> 5.77 us
    unnamed x12 -> x10, local copies, waits for them, and re-layouts: 0.66 us -> 0.02 us
    ppermute x4, starting transfers between devices: 21.2 us -> 21.6 us  [exchange(): lax.ppermute(z, 'row', [(s, targets(s)) for s in range(devices) if target...]
    all_gather x1, blocking collectives: 5.41 us -> 5.77 us  [on_device(): full = lax.all_gather(panel, 'col', axis=0, tiled=True)]
where the time goes in v4:
time: 30.9 us; the launch traced here: 30.7 us
  starting transfers between devices  21.6 us (70%)
  blocking collectives  5.77 us (19%)
  Pallas kernels  2.33 us (8%)
  waiting for transfers between devices  0.89 us (3%)
    ppermute x4, starting transfers between devices, exchange(): lax.ppermute(z, 'row', [(s, targets(s)) for s in range(devices) if target...  21.6 us
    all_gather x1, blocking collectives, on_device(): full = lax.all_gather(panel, 'col', axis=0, tiled=True)  5.77 us
    pallas_call x1, Pallas kernels, on_device(): pl.pallas_call(transform_kernel, out_shape=(jax.ShapeDtypeStruct((outs, n...  1.34 us
    pallas_call x1, Pallas kernels, on_device(): pl.pallas_call(finish_kernel, out_shape=jax.ShapeDtypeStruct((outs, nodes...  0.91 us
    ppermute x4, waiting for transfers between devices, exchange(): lax.ppermute(z, 'row', [(s, targets(s)) for s in range(devices) if target...  0.89 us
  transfers between devices with their start and end apart: 4, of which 1 were waited for; matrix products, arithmetic and copies ran while one was open for 0% of the time, Pallas kernels for 0%

profile of v4, /device:TPU:56, one launch (start us, length us, event | category | flops | bytes accessed | tf_op | source)
XLA Modules:
  0.0 30.7 jit_solution(3450516771180492723)
XLA Ops:
  0.0 0.0 copy-start.3
  0.0 0.0 copy-start.2
  0.0 0.0 copy-start
  0.0 0.0 copy-start.4
  0.0 0.0 copy-start.1
  0.0 0.1 clear.1
  0.1 5.8 %all_gather.3.full_ref = bf16[256,256]{1,0:T(8,128)(2,1)S(1)} all-gather(bf16[64,256]{1,0:T(8,128)(2,1)} %bitcast.6), channel_id=1, replica_groups=mesh['row'=192,'col'=4] {'col'}, dimensions={0}, use_global_device_ids=true | all-gather | bytes 163840 | tf_op jit(solution)/shard_map/all_gather | solution.py:109
  5.9 0.0 copy-done.3
  5.9 0.0 copy-done.2
  5.9 0.0 copy-done
  5.9 0.0 copy-done.4
  5.9 0.0 copy-done.1
  5.9 1.3 %transform.1 = (bf16[64,256]{1,0:T(8,128)(2,1)S(1)}, bf16[9,128,128]{2,1,0:T(8,128)(2,1)S(1)}, bf16[9,128,128]{2,1,0:T(8,128)(2,1)S(1)}, f32[8,256]{1,0:T(8,128)S(1)}, f32[64,1]{1,0:T(8,128)S(1)}) custom-call(s32[2]{0:T(128)S(1)} %copy-done.3, s32[2,32]{1,0:T(2,128)S(1)} %copy-done.2, ...), custom_call_target="tpu_custom_call", output_to_operand_aliasing={{1}: (6, {}), {2}: (7, {})} | custom-call | tf_op jit(solution)/shard_map/transform/pallas_call | solution.py:110
  7.3 3.9 %collective-permute-start.3 = (bf16[64,256]{1,0:T(8,128)(2,1)S(1)}, bf16[64,256]{1,0:T(8,128)(2,1)S(1)}, u32[]{:S(2)}, u32[]{:S(2)}) collective-permute-start(bf16[64,256]{1,0:T(8,128)(2,1)S(1)} %get-tuple-element.20.z_ref), channel_id=1, source_target_pairs={{0,4},{4,8},{8,12},{12,16},{16,20},{20,24},{24,28},{28,32},{32,36}... | collective-permute-start | bytes 98312 | tf_op jit(solution)/shard_map/ppermute | solution.py:127
  11.2 5.1 %collective-permute-start.2 = (bf16[64,256]{1,0:T(8,128)(2,1)S(1)}, bf16[64,256]{1,0:T(8,128)(2,1)S(1)}, u32[]{:S(2)}, u32[]{:S(2)}) collective-permute-start(bf16[64,256]{1,0:T(8,128)(2,1)S(1)} %get-tuple-element.20.z_ref), channel_id=1, source_target_pairs={{0,384},{4,388},{8,392},{12,396},{16,400},{20,404},{48,432},{52,43... | collective-permute-start | bytes 98312 | tf_op jit(solution)/shard_map/ppermute | solution.py:127
  16.3 11.9 %collective-permute-start.1 = (bf16[64,256]{1,0:T(8,128)(2,1)S(1)}, bf16[64,256]{1,0:T(8,128)(2,1)S(1)}, u32[]{:S(2)}, u32[]{:S(2)}) collective-permute-start(bf16[64,256]{1,0:T(8,128)(2,1)S(1)} %get-tuple-element.20.z_ref), channel_id=1, source_target_pairs={{4,0},{8,4},{12,8},{16,12},{20,16},{24,20},{28,24},{32,28},{36,32}... | collective-permute-start | bytes 98312 | tf_op jit(solution)/shard_map/ppermute | solution.py:127
  28.2 0.7 %collective-permute-start = (bf16[64,256]{1,0:T(8,128)(2,1)S(1)}, bf16[64,256]{1,0:T(8,128)(2,1)S(1)}, u32[]{:S(2)}, u32[]{:S(2)}) collective-permute-start(bf16[64,256]{1,0:T(8,128)(2,1)S(1)} %get-tuple-element.20.z_ref), channel_id=1, source_target_pairs={{24,408},{28,412},{32,416},{36,420},{40,424},{44,428},{72,456},{76... | collective-permute-start | bytes 98312 | tf_op jit(solution)/shard_map/ppermute | solution.py:127
  28.9 0.0 collective-permute-done.3.before_ref
  28.9 0.0 collective-permute-done.2.first_ref
  28.9 0.9 %collective-permute-done.1.after_ref = bf16[64,256]{1,0:T(8,128)(2,1)S(1)} collective-permute-done((bf16[64,256]{1,0:T(8,128)(2,1)S(1)}, bf16[64,256]{1,0:T(8,128)(2,1)S(1)}, u32[]{:S(2)}, u32[]{:S(2)}) %collective-permute-start.1) | collective-permute-done | bytes 32800 | tf_op jit(solution)/shard_map/ppermute | solution.py:127
  29.8 0.0 collective-permute-done.last_ref
  29.8 0.9 %finish.1 = bf16[64,256]{1,0:T(8,128)(2,1)} custom-call(bf16[64,256]{1,0:T(8,128)(2,1)S(1)} %collective-permute-done.last_ref, bf16[64,256]{1,0:T(8,128)(2,1)S(1)} %collective-permute-done.1.after_ref, bf16[64,256]{1,0:T(8,128)(2,1)S(1)} %collective-permute-done.2.first_ref, bf16[64,256]{1,0:T(8,128)(2,1)S(1)} %collective-permute-done.3.before_ref, ...), custom_call_target="tpu_custom_call" | custom-call | tf_op jit(solution)/shard_map/finish/pallas_call | solution.py:144
Async XLA Ops:
  0.0 5.9 %copy-start.3 = (s32[2]{0:T(128)S(1)}, s32[2]{0:T(128)}, u32[]{:S(2)}) copy-start(s32[2]{0:T(128)} %count_ref.1) | copy-start | bytes 28
  0.0 5.9 %copy-start.2 = (s32[2,32]{1,0:T(2,128)S(1)}, s32[2,32]{1,0:T(2,128)}, u32[]{:S(2)}) copy-start(s32[2,32]{1,0:T(2,128)} %cols_ref.1) | copy-start | bytes 772
  0.0 5.9 %copy-start = (bf16[2,32,128,128]{3,2,1,0:T(8,128)(2,1)S(1)}, bf16[2,32,128,128]{3,2,1,0:T(8,128)(2,1)}, u32[]{:S(2)}) copy-start(bf16[2,32,128,128]{3,2,1,0:T(8,128)(2,1)} %tiles.1) | copy-start | bytes 6291460
  0.0 5.9 %copy-start.4 = (f32[64]{0:T(128)S(1)}, f32[64]{0:T(128)}, u32[]{:S(2)}) copy-start(f32[64]{0:T(128)} %param.8) | copy-start | bytes 772
  0.0 5.9 %copy-start.1 = (bf16[256,64]{0,1:T(8,128)(2,1)S(1)}, bf16[256,64]{0,1:T(8,128)(2,1)}, u32[]{:S(2)}) copy-start(bf16[256,64]{0,1:T(8,128)(2,1)} %param.7) | copy-start | bytes 98308
  7.3 21.6 %collective-permute-start.3 = (bf16[64,256]{1,0:T(8,128)(2,1)S(1)}, bf16[64,256]{1,0:T(8,128)(2,1)S(1)}, u32[]{:S(2)}, u32[]{:S(2)}) collective-permute-start(bf16[64,256]{1,0:T(8,128)(2,1)S(1)} %get-tuple-element.20.z_ref), channel_id=1, source_target_pairs={{0,4},{4,8},{8,12},{12,16},{16,20},{20,24},{24,28},{28,32},{32,36}... | collective-permute-start | bytes 98312 | tf_op jit(solution)/shard_map/ppermute | solution.py:127
  11.2 17.8 %collective-permute-start.2 = (bf16[64,256]{1,0:T(8,128)(2,1)S(1)}, bf16[64,256]{1,0:T(8,128)(2,1)S(1)}, u32[]{:S(2)}, u32[]{:S(2)}) collective-permute-start(bf16[64,256]{1,0:T(8,128)(2,1)S(1)} %get-tuple-element.20.z_ref), channel_id=1, source_target_pairs={{0,384},{4,388},{8,392},{12,396},{16,400},{20,404},{48,432},{52,43... | collective-permute-start | bytes 98312 | tf_op jit(solution)/shard_map/ppermute | solution.py:127
  16.3 13.5 %collective-permute-start.1 = (bf16[64,256]{1,0:T(8,128)(2,1)S(1)}, bf16[64,256]{1,0:T(8,128)(2,1)S(1)}, u32[]{:S(2)}, u32[]{:S(2)}) collective-permute-start(bf16[64,256]{1,0:T(8,128)(2,1)S(1)} %get-tuple-element.20.z_ref), channel_id=1, source_target_pairs={{4,0},{8,4},{12,8},{16,12},{20,16},{24,20},{28,24},{32,28},{36,32}... | collective-permute-start | bytes 98312 | tf_op jit(solution)/shard_map/ppermute | solution.py:127
  28.2 1.6 %collective-permute-start = (bf16[64,256]{1,0:T(8,128)(2,1)S(1)}, bf16[64,256]{1,0:T(8,128)(2,1)S(1)}, u32[]{:S(2)}, u32[]{:S(2)}) collective-permute-start(bf16[64,256]{1,0:T(8,128)(2,1)S(1)} %get-tuple-element.20.z_ref), channel_id=1, source_target_pairs={{24,408},{28,412},{32,416},{36,420},{40,424},{44,428},{72,456},{76... | collective-permute-start | bytes 98312 | tf_op jit(solution)/shard_map/ppermute | solution.py:127

commit v5 on v4

v5 whole, which is shorter than its diff:
```python
import functools

import jax
import jax.numpy as jnp
from jax import lax
from jax.experimental import pallas as pl
from jax.experimental.pallas import tpu as pltpu
from jax.sharding import PartitionSpec as P

F32 = jnp.float32
BF16 = jnp.bfloat16
VMEM = pltpu.MemorySpace.VMEM
NT = (((1,), (1,)), ((), ()))
LINE = 12
NEAR = 6
UNROLL = 3


def split(value):
    high = value.astype(BF16)
    return high, (value - high.astype(F32)).astype(BF16)


def clear_kernel(*out_refs):
    for ref in out_refs:
        ref[...] = jnp.zeros_like(ref)


def transform_kernel(count_ref, tiles, full_ref, weight_ref, z_ref, scale_ref):
    own_rows, kmax, bsize, _ = tiles.shape
    product = jnp.dot(weight_ref[...], full_ref[...], preferred_element_type=F32)
    sums = []
    for r in range(own_rows):
        count = jnp.broadcast_to(count_ref[:, r : r + 1], (8, bsize))
        total = jnp.zeros((bsize // 8, 8, bsize), F32)
        for k in range(kmax):
            live = jnp.where(count > k, 1.0, 0.0)
            total += tiles[r, k].astype(F32).reshape(total.shape) * live[None]
        sums.append(total.reshape(bsize, bsize))
    parts = jnp.concatenate(split(jnp.concatenate(sums, axis=0)), axis=1)
    ones = jnp.ones((16, 2 * bsize), BF16)
    degree = 1.0 + lax.dot_general(ones, parts, NT, preferred_element_type=F32)
    scale = lax.rsqrt(degree[:1, :])
    z_ref[...] = (product * scale).astype(BF16)
    scale_ref[...] = jnp.broadcast_to(scale, scale_ref.shape)


def square(blocks, slot):
    rows = [jnp.concatenate([ref[2 * slot], ref[2 * slot + 1]], axis=1) for ref in blocks]
    return jnp.concatenate(rows, axis=0)


def blocks_kernel(mine, count_any, cols_any, tiles, z_ref, bias_ref, *refs):
    upper_ref, lower_ref, base_ref, offset_ref, same_ref, count_ref, cols_ref, sems = refs[-8:]
    same_ref[...] = z_ref[...]

    @pl.when(mine(lax.rem(lax.axis_index("row"), LINE)))
    def _():
        loads = [
            pltpu.make_async_copy(count_any, count_ref, sems.at[0]),
            pltpu.make_async_copy(cols_any, cols_ref, sems.at[1]),
        ]
        for load in loads:
            load.start()
        for load in loads:
            load.wait()
        blocks = (upper_ref, lower_ref)
        own_rows = tiles.shape[0]
        first = lax.axis_index("row") * own_rows - 2
        spare = upper_ref.shape[0] - 1
        counts = [count_ref[r] for r in range(own_rows)]

        def add(r, k):
            place = jnp.where(k < counts[r], jnp.clip(cols_ref[r, k] - first, 0, 5), spare)
            blocks[r][place] += tiles[r, k]

        for r in range(own_rows):
            blocks[r][6 + r] = tiles[r, 1]
            add(r, 0)

        def step(k, _):
            for u in range(UNROLL):
                for r in range(own_rows):
                    add(r, 2 + k * UNROLL + u)
            return 0

        longest = jnp.maximum(counts[0], counts[1])
        lax.fori_loop(0, (longest - 2 + UNROLL - 1) // UNROLL, step, 0)
        own = z_ref[...]
        base_ref[...] = own.astype(F32) + lax.dot_general(own, square(blocks, 1), NT, preferred_element_type=F32)
        outs = bias_ref.shape[1]
        eye = lax.broadcasted_iota(jnp.int32, (outs, outs), 0) == lax.broadcasted_iota(jnp.int32, (outs, outs), 1)
        offset_ref[...] = jnp.sum(jnp.where(eye, bias_ref[...], 0.0), axis=1, keepdims=True)


def finish_kernel(
    last_ref, after_ref, first_ref, before_ref, upper_ref, lower_ref, base_ref, scale_ref, offset_ref, out_ref
):
    blocks = (upper_ref, lower_ref)
    total = base_ref[...]
    pair = first_ref[...] + last_ref[...]
    for slot, z in ((0, before_ref[...]), (2, after_ref[...]), (3, pair)):
        total += lax.dot_general(z, square(blocks, slot), NT, preferred_element_type=F32)
    result = scale_ref[:1, :] * total + offset_ref[...]
    out_ref[...] = jnp.maximum(result, 0.0).astype(BF16)


def on_device(features, weight, bias, adjacency, block_cols, block_count):
    own_rows, _, bsize, _ = adjacency.shape
    devices = lax.axis_size("row")
    nodes = features.shape[0]
    outs = weight.shape[1]
    vmem = pl.BlockSpec(memory_space=VMEM)
    anywhere = pl.BlockSpec(memory_space=pl.ANY)

    sums = jax.ShapeDtypeStruct((9, bsize, bsize), BF16)
    cleared = pl.pallas_call(
        clear_kernel,
        out_shape=(sums,) * own_rows,
        out_specs=(vmem,) * own_rows,
        compiler_params=pltpu.CompilerParams(vmem_limit_bytes=4 << 20),
        cost_estimate=pl.CostEstimate(flops=550_000_000, bytes_accessed=1 << 20, transcendentals=0),
        name="clear",
    )()
    panel, cleared = lax.optimization_barrier((features.T, cleared))
    full = lax.all_gather(panel, "col", axis=0, tiled=True)
    z, scale = pl.pallas_call(
        transform_kernel,
        out_shape=(
            jax.ShapeDtypeStruct((outs, nodes), BF16),
            jax.ShapeDtypeStruct((8, nodes), F32),
        ),
        in_specs=[vmem] * 4,
        out_specs=(vmem,) * 2,
        compiler_params=pltpu.CompilerParams(vmem_limit_bytes=12 << 20),
        name="transform",
    )(block_count.reshape(1, -1), adjacency, full, weight.T)

    half = devices // 2

    def plus(s):
        return s + 1 if s + 1 < devices else None

    def minus(s):
        return s - 1 if s > 0 else None

    def pair(s):
        return (s + half) % devices

    def sum_blocks(mine, values, kept):
        shapes = (
            sums,
            sums,
            jax.ShapeDtypeStruct((outs, nodes), F32),
            jax.ShapeDtypeStruct((outs, 1), F32),
            jax.ShapeDtypeStruct((outs, nodes), BF16),
        )
        return pl.pallas_call(
            functools.partial(blocks_kernel, mine),
            out_shape=shapes,
            in_specs=[anywhere, anywhere] + [vmem] * (3 + len(kept)),
            input_output_aliases={5 + i: i for i in range(len(kept))},
            out_specs=(vmem,) * 5,
            scratch_shapes=[
                pltpu.SMEM(block_count.shape, jnp.int32),
                pltpu.SMEM(block_cols.shape, jnp.int32),
                pltpu.SemaphoreType.DMA((2,)),
            ],
            compiler_params=pltpu.CompilerParams(vmem_limit_bytes=12 << 20),
            cost_estimate=pl.CostEstimate(flops=50_000_000, bytes_accessed=3 << 20, transcendentals=0),
            name="blocks",
        )(block_count, block_cols, adjacency, values, bias.reshape(1, -1), *kept)

    *kept, z = sum_blocks(lambda place: place < NEAR, z, cleared)

    def exchange(targets):
        return lax.ppermute(z, "row", [(s, targets(s)) for s in range(devices) if targets(s) is not None])

    before = exchange(plus)
    first = exchange(lambda s: pair(s) if s % LINE < NEAR or (s >= half and s % LINE < LINE - 1) else None)
    after = exchange(minus)
    last = exchange(lambda s: pair(s) if s % LINE == LINE - 1 or (s < half and s % LINE >= NEAR) else None)
    upper, lower, base, offset, _ = sum_blocks(lambda place: place >= NEAR, z, kept)
    out = pl.pallas_call(
        finish_kernel,
        out_shape=jax.ShapeDtypeStruct((outs, nodes), BF16),
        in_specs=[vmem] * 9,
        out_specs=vmem,
        compiler_params=pltpu.CompilerParams(vmem_limit_bytes=4 << 20),
        name="finish",
    )(last, after, first, before, upper, lower, base, scale, offset)
    return out.T


def solution(mesh):
    return jax.shard_map(
        on_device,
        mesh=mesh,
        in_specs=(
            P("row", "col"),
            P(None, "col"),
            P("col"),
            P("row", None, None, None),
            P("row", None),
            P("row"),
        ),
        out_specs=P("row", "col"),
        check_vma=False,
    )
```

time: 30.9 us -> 30.3 us (0.981)
  starting transfers between devices: 21.6 us -> 20.7 us
  Pallas kernels: 2.33 us -> 3.14 us
  waiting for transfers between devices: 0.89 us -> 0.22 us
    pallas_call x0 -> x2, Pallas kernels: none -> 1.57 us  [sum_blocks(): pl.pallas_call(functools.partial(blocks_kernel, mine), out_shape=shapes,...]
    ppermute x4, starting transfers between devices: 21.6 us -> 20.7 us  [exchange(): lax.ppermute(z, 'row', [(s, targets(s)) for s in range(devices) if target...]
    pallas_call x1, Pallas kernels: 1.34 us -> 0.6 us  [on_device(): pl.pallas_call(transform_kernel, out_shape=(jax.ShapeDtypeStruct((outs, n...]
    ppermute x4, waiting for transfers between devices: 0.89 us -> 0.22 us  [exchange(): lax.ppermute(z, 'row', [(s, targets(s)) for s in range(devices) if target...]
  transfers between devices with their start and end apart: 4 -> 4, of which waited for: 1 -> 1; matrix products, arithmetic and copies ran while one was open for 0% -> 0% of each run, Pallas kernels for 0% -> 2%
where the time goes in v5:
time: 30.3 us; the launch traced here: 30 us
  starting transfers between devices  20.7 us (68%)
  blocking collectives  5.77 us (19%)
  Pallas kernels  3.14 us (10%)
    ppermute x4, starting transfers between devices, exchange(): lax.ppermute(z, 'row', [(s, targets(s)) for s in range(devices) if target...  20.7 us
    all_gather x1, blocking collectives, on_device(): full = lax.all_gather(panel, 'col', axis=0, tiled=True)  5.77 us
    pallas_call x2, Pallas kernels, sum_blocks(): pl.pallas_call(functools.partial(blocks_kernel, mine), out_shape=shapes,...  1.57 us
    pallas_call x1, Pallas kernels, on_device(): pl.pallas_call(finish_kernel, out_shape=jax.ShapeDtypeStruct((outs, nodes...  0.89 us
  transfers between devices with their start and end apart: 4, of which 1 were waited for; matrix products, arithmetic and copies ran while one was open for 0% of the time, Pallas kernels for 2%

profile of v5, /device:TPU:56, one launch (start us, length us, event | category | flops | bytes accessed | tf_op | source)
XLA Modules:
  0.0 30.0 jit_solution(1996772612662108142)
XLA Ops:
  0.0 0.0 copy-start
  0.0 0.0 copy-start.2
  0.0 0.0 copy-start.1
  0.0 0.0 copy-start.3
  0.0 0.0 copy-start.4
  0.0 0.1 clear.1
  0.1 5.8 %all_gather.3.full_ref = bf16[256,256]{1,0:T(8,128)(2,1)S(1)} all-gather(bf16[64,256]{1,0:T(8,128)(2,1)} %bitcast.9), channel_id=1, replica_groups=mesh['row'=192,'col'=4] {'col'}, dimensions={0}, use_global_device_ids=true | all-gather | bytes 163840 | tf_op jit(solution)/shard_map/all_gather | solution.py:126
  5.9 0.0 copy-done
  5.9 0.0 copy-done.2
  5.9 0.0 copy-done.1
  5.9 0.6 %transform.1 = (bf16[64,256]{1,0:T(8,128)(2,1)S(1)}, f32[8,256]{1,0:T(8,128)S(1)}) custom-call(s32[1,2]{1,0:T(1,128)S(1)} %bitcast.6, bf16[2,32,128,128]{3,2,1,0:T(8,128)(2,1)S(1)} %copy-done, bf16[256,256]{1,0:T(8,128)(2,1)S(1)} %all_gather.3.full_ref, bf16[64,256]{1,0:T(8,128)(2,1)S(1)} %bitcast.5), custom_call_target="tpu_custom_call" | custom-call | tf_op jit(solution)/shard_map/transform/pallas_call | solution.py:127
  6.5 0.0 copy-done.3
  6.5 0.0 copy-done.4
  6.6 0.9 %blocks.2 = (bf16[9,128,128]{2,1,0:T(8,128)(2,1)S(1)}, bf16[9,128,128]{2,1,0:T(8,128)(2,1)S(1)}, f32[64,256]{1,0:T(8,128)S(1)}, f32[64,1]{1,0:T(8,128)S(1)}, bf16[64,256]{1,0:T(8,128)(2,1)S(1)}) custom-call(s32[2]{0:T(128)S(1)} %copy-done.2, s32[2,32]{1,0:T(2,128)S(1)} %copy-done.3, ...), custom_call_target="tpu_custom_call", output_to_operand_aliasing={{0}: (5, {}), {1}: (6, {})} | custom-call | flops 50000000 | bytes 3145728 | tf_op jit(solution)/shard_map/blocks/pallas_call | solution.py:158
  7.5 4.7 %collective-permute-start.3 = (bf16[64,256]{1,0:T(8,128)(2,1)S(1)}, bf16[64,256]{1,0:T(8,128)(2,1)S(1)}, u32[]{:S(2)}, u32[]{:S(2)}) collective-permute-start(bf16[64,256]{1,0:T(8,128)(2,1)S(1)} %get-tuple-element.27.z_ref), channel_id=1, source_target_pairs={{0,4},{4,8},{8,12},{12,16},{16,20},{20,24},{24,28},{28,32},{32,36}... | collective-permute-start | bytes 98312 | tf_op jit(solution)/shard_map/ppermute | solution.py:177
  12.2 4.3 %collective-permute-start.2 = (bf16[64,256]{1,0:T(8,128)(2,1)S(1)}, bf16[64,256]{1,0:T(8,128)(2,1)S(1)}, u32[]{:S(2)}, u32[]{:S(2)}) collective-permute-start(bf16[64,256]{1,0:T(8,128)(2,1)S(1)} %get-tuple-element.27.z_ref), channel_id=1, source_target_pairs={{0,384},{4,388},{8,392},{12,396},{16,400},{20,404},{48,432},{52,43... | collective-permute-start | bytes 98312 | tf_op jit(solution)/shard_map/ppermute | solution.py:177
  16.5 11.1 %collective-permute-start.1 = (bf16[64,256]{1,0:T(8,128)(2,1)S(1)}, bf16[64,256]{1,0:T(8,128)(2,1)S(1)}, u32[]{:S(2)}, u32[]{:S(2)}) collective-permute-start(bf16[64,256]{1,0:T(8,128)(2,1)S(1)} %get-tuple-element.27.z_ref), channel_id=1, source_target_pairs={{4,0},{8,4},{12,8},{16,12},{20,16},{24,20},{28,24},{32,28},{36,32}... | collective-permute-start | bytes 98312 | tf_op jit(solution)/shard_map/ppermute | solution.py:177
  27.6 0.7 %collective-permute-start = (bf16[64,256]{1,0:T(8,128)(2,1)S(1)}, bf16[64,256]{1,0:T(8,128)(2,1)S(1)}, u32[]{:S(2)}, u32[]{:S(2)}) collective-permute-start(bf16[64,256]{1,0:T(8,128)(2,1)S(1)} %get-tuple-element.27.z_ref), channel_id=1, source_target_pairs={{24,408},{28,412},{32,416},{36,420},{40,424},{44,428},{72,456},{76... | collective-permute-start | bytes 98312 | tf_op jit(solution)/shard_map/ppermute | solution.py:177
  28.2 0.7 %blocks.3 = (bf16[9,128,128]{2,1,0:T(8,128)(2,1)S(1)}, bf16[9,128,128]{2,1,0:T(8,128)(2,1)S(1)}, f32[64,256]{1,0:T(8,128)S(1)}, f32[64,1]{1,0:T(8,128)S(1)}, bf16[64,256]{1,0:T(8,128)(2,1)}) custom-call(s32[2]{0:T(128)S(1)} %copy-done.2, s32[2,32]{1,0:T(2,128)S(1)} %copy-done.3, ...), custom_call_target="tpu_custom_call", output_to_operand_aliasing={{0}: (5, {}), {1}: (6, {}), {2}: (7, {}), {3}: (8, {})} | custom-call | flops 50000000 | bytes 3145728 | tf_op jit(solution)/shard_map/blocks/pallas_call | solution.py:158
  28.9 0.0 collective-permute-done.3.before_ref
  28.9 0.0 collective-permute-done.2.first_ref
  28.9 0.2 collective-permute-done.1.after_ref
  29.1 0.0 collective-permute-done.last_ref
  29.2 0.9 %finish.1 = bf16[64,256]{1,0:T(8,128)(2,1)} custom-call(bf16[64,256]{1,0:T(8,128)(2,1)S(1)} %collective-permute-done.last_ref, bf16[64,256]{1,0:T(8,128)(2,1)S(1)} %collective-permute-done.1.after_ref, bf16[64,256]{1,0:T(8,128)(2,1)S(1)} %collective-permute-done.2.first_ref, bf16[64,256]{1,0:T(8,128)(2,1)S(1)} %collective-permute-done.3.before_ref, ...), custom_call_target="tpu_custom_call" | custom-call | tf_op jit(solution)/shard_map/finish/pallas_call | solution.py:184
Async XLA Ops:
  0.0 5.9 %copy-start = (bf16[2,32,128,128]{3,2,1,0:T(8,128)(2,1)S(1)}, bf16[2,32,128,128]{3,2,1,0:T(8,128)(2,1)}, u32[]{:S(2)}) copy-start(bf16[2,32,128,128]{3,2,1,0:T(8,128)(2,1)} %tiles.5) | copy-start | bytes 6291460
  0.0 5.9 %copy-start.2 = (s32[2]{0:T(128)S(1)}, s32[2]{0:T(128)}, u32[]{:S(2)}) copy-start(s32[2]{0:T(128)} %count_any.3) | copy-start | bytes 28
  0.0 5.9 %copy-start.1 = (bf16[256,64]{0,1:T(8,128)(2,1)S(1)}, bf16[256,64]{0,1:T(8,128)(2,1)}, u32[]{:S(2)}) copy-start(bf16[256,64]{0,1:T(8,128)(2,1)} %param.7) | copy-start | bytes 98308
  0.0 6.5 %copy-start.3 = (s32[2,32]{1,0:T(2,128)S(1)}, s32[2,32]{1,0:T(2,128)}, u32[]{:S(2)}) copy-start(s32[2,32]{1,0:T(2,128)} %cols_any.3) | copy-start | bytes 772
  0.0 6.5 %copy-start.4 = (f32[64]{0:T(128)S(1)}, f32[64]{0:T(128)}, u32[]{:S(2)}) copy-start(f32[64]{0:T(128)} %param.8) | copy-start | bytes 772
  7.5 21.4 %collective-permute-start.3 = (bf16[64,256]{1,0:T(8,128)(2,1)S(1)}, bf16[64,256]{1,0:T(8,128)(2,1)S(1)}, u32[]{:S(2)}, u32[]{:S(2)}) collective-permute-start(bf16[64,256]{1,0:T(8,128)(2,1)S(1)} %get-tuple-element.27.z_ref), channel_id=1, source_target_pairs={{0,4},{4,8},{8,12},{12,16},{16,20},{20,24},{24,28},{28,32},{32,36}... | collective-permute-start | bytes 98312 | tf_op jit(solution)/shard_map/ppermute | solution.py:177
  12.2 16.8 %collective-permute-start.2 = (bf16[64,256]{1,0:T(8,128)(2,1)S(1)}, bf16[64,256]{1,0:T(8,128)(2,1)S(1)}, u32[]{:S(2)}, u32[]{:S(2)}) collective-permute-start(bf16[64,256]{1,0:T(8,128)(2,1)S(1)} %get-tuple-element.27.z_ref), channel_id=1, source_target_pairs={{0,384},{4,388},{8,392},{12,396},{16,400},{20,404},{48,432},{52,43... | collective-permute-start | bytes 98312 | tf_op jit(solution)/shard_map/ppermute | solution.py:177
  16.5 12.7 %collective-permute-start.1 = (bf16[64,256]{1,0:T(8,128)(2,1)S(1)}, bf16[64,256]{1,0:T(8,128)(2,1)S(1)}, u32[]{:S(2)}, u32[]{:S(2)}) collective-permute-start(bf16[64,256]{1,0:T(8,128)(2,1)S(1)} %get-tuple-element.27.z_ref), channel_id=1, source_target_pairs={{4,0},{8,4},{12,8},{16,12},{20,16},{24,20},{28,24},{32,28},{36,32}... | collective-permute-start | bytes 98312 | tf_op jit(solution)/shard_map/ppermute | solution.py:177
  27.6 1.6 %collective-permute-start = (bf16[64,256]{1,0:T(8,128)(2,1)S(1)}, bf16[64,256]{1,0:T(8,128)(2,1)S(1)}, u32[]{:S(2)}, u32[]{:S(2)}) collective-permute-start(bf16[64,256]{1,0:T(8,128)(2,1)S(1)} %get-tuple-element.27.z_ref), channel_id=1, source_target_pairs={{24,408},{28,412},{32,416},{36,420},{40,424},{44,428},{72,456},{76... | collective-permute-start | bytes 98312 | tf_op jit(solution)/shard_map/ppermute | solution.py:177

commit v6 on v5

--- a/solution.py
+++ b/solution.py
@@ -50,8 +50,8 @@
     return jnp.concatenate(rows, axis=0)
 
 
-def blocks_kernel(mine, count_any, cols_any, tiles, z_ref, bias_ref, *refs):
-    upper_ref, lower_ref, base_ref, offset_ref, same_ref, count_ref, cols_ref, sems = refs[-8:]
+def blocks_kernel(mine, count_any, cols_any, tiles_any, z_ref, bias_ref, *refs):
+    upper_ref, lower_ref, base_ref, offset_ref, same_ref, count_ref, cols_ref, tiles, sems = refs[-9:]
     same_ref[...] = z_ref[...]
 
     @pl.when(mine(lax.rem(lax.axis_index("row"), LINE)))
@@ -59,6 +59,7 @@
         loads = [
             pltpu.make_async_copy(count_any, count_ref, sems.at[0]),
             pltpu.make_async_copy(cols_any, cols_ref, sems.at[1]),
+            pltpu.make_async_copy(tiles_any, tiles, sems.at[2]),
         ]
         for load in loads:
             load.start()
@@ -158,13 +159,14 @@
         return pl.pallas_call(
             functools.partial(blocks_kernel, mine),
             out_shape=shapes,
-            in_specs=[anywhere, anywhere] + [vmem] * (3 + len(kept)),
+            in_specs=[anywhere] * 3 + [vmem] * (2 + len(kept)),
             input_output_aliases={5 + i: i for i in range(len(kept))},
             out_specs=(vmem,) * 5,
             scratch_shapes=[
                 pltpu.SMEM(block_count.shape, jnp.int32),
                 pltpu.SMEM(block_cols.shape, jnp.int32),
-                pltpu.SemaphoreType.DMA((2,)),
+                pltpu.VMEM(adjacency.shape, BF16),
+                pltpu.SemaphoreType.DMA((3,)),
             ],
             compiler_params=pltpu.CompilerParams(vmem_limit_bytes=12 << 20),
             cost_estimate=pl.CostEstimate(flops=50_000_000, bytes_accessed=3 << 20, transcendentals=0),

time: 30.3 us -> 30.3 us (level)
  no operation moved by 1% of the time
where the time goes in v6:
time: 30.3 us; the launch traced here: 30.1 us
  starting transfers between devices  20.8 us (69%)
  blocking collectives  5.77 us (19%)
  Pallas kernels  3.11 us (10%)
    ppermute x4, starting transfers between devices, exchange(): lax.ppermute(z, 'row', [(s, targets(s)) for s in range(devices) if target...  20.8 us
    all_gather x1, blocking collectives, on_device(): full = lax.all_gather(panel, 'col', axis=0, tiled=True)  5.77 us
    pallas_call x2, Pallas kernels, sum_blocks(): pl.pallas_call(functools.partial(blocks_kernel, mine), out_shape=shapes,...  1.54 us
    pallas_call x1, Pallas kernels, on_device(): pl.pallas_call(finish_kernel, out_shape=jax.ShapeDtypeStruct((outs, nodes...  0.89 us
  transfers between devices with their start and end apart: 4, of which 1 were waited for; matrix products, arithmetic and copies ran while one was open for 0% of the time, Pallas kernels for 2%

profile of v6, /device:TPU:56, one launch (start us, length us, event | category | flops | bytes accessed | tf_op | source)
XLA Modules:
  0.0 30.1 jit_solution(10865515964911551324)
XLA Ops:
  0.0 0.0 copy-start
  0.0 0.0 copy-start.2
  0.0 0.0 copy-start.1
  0.0 0.0 copy-start.3
  0.0 0.0 copy-start.4
  0.0 0.1 clear.1
  0.1 5.8 %all_gather.3.full_ref = bf16[256,256]{1,0:T(8,128)(2,1)S(1)} all-gather(bf16[64,256]{1,0:T(8,128)(2,1)} %bitcast.9), channel_id=1, replica_groups=mesh['row'=192,'col'=4] {'col'}, dimensions={0}, use_global_device_ids=true | all-gather | bytes 163840 | tf_op jit(solution)/shard_map/all_gather | solution.py:127
  5.9 0.0 copy-done
  5.9 0.0 copy-done.2
  5.9 0.0 copy-done.1
  5.9 0.6 %transform.1 = (bf16[64,256]{1,0:T(8,128)(2,1)S(1)}, f32[8,256]{1,0:T(8,128)S(1)}) custom-call(s32[1,2]{1,0:T(1,128)S(1)} %bitcast.6, bf16[2,32,128,128]{3,2,1,0:T(8,128)(2,1)S(1)} %copy-done, bf16[256,256]{1,0:T(8,128)(2,1)S(1)} %all_gather.3.full_ref, bf16[64,256]{1,0:T(8,128)(2,1)S(1)} %bitcast.5), custom_call_target="tpu_custom_call" | custom-call | tf_op jit(solution)/shard_map/transform/pallas_call | solution.py:128
  6.5 0.0 copy-done.3
  6.5 0.0 copy-done.4
  6.6 0.9 %blocks.2 = (bf16[9,128,128]{2,1,0:T(8,128)(2,1)S(1)}, bf16[9,128,128]{2,1,0:T(8,128)(2,1)S(1)}, f32[64,256]{1,0:T(8,128)S(1)}, f32[64,1]{1,0:T(8,128)S(1)}, bf16[64,256]{1,0:T(8,128)(2,1)S(1)}) custom-call(s32[2]{0:T(128)S(1)} %copy-done.2, s32[2,32]{1,0:T(2,128)S(1)} %copy-done.3, ...), custom_call_target="tpu_custom_call", output_to_operand_aliasing={{0}: (5, {}), {1}: (6, {})} | custom-call | flops 50000000 | bytes 3145728 | tf_op jit(solution)/shard_map/blocks/pallas_call | solution.py:159
  7.4 4.3 %collective-permute-start.3 = (bf16[64,256]{1,0:T(8,128)(2,1)S(1)}, bf16[64,256]{1,0:T(8,128)(2,1)S(1)}, u32[]{:S(2)}, u32[]{:S(2)}) collective-permute-start(bf16[64,256]{1,0:T(8,128)(2,1)S(1)} %get-tuple-element.27.z_ref), channel_id=1, source_target_pairs={{0,4},{4,8},{8,12},{12,16},{16,20},{20,24},{24,28},{28,32},{32,36}... | collective-permute-start | bytes 98312 | tf_op jit(solution)/shard_map/ppermute | solution.py:179
  11.8 4.7 %collective-permute-start.2 = (bf16[64,256]{1,0:T(8,128)(2,1)S(1)}, bf16[64,256]{1,0:T(8,128)(2,1)S(1)}, u32[]{:S(2)}, u32[]{:S(2)}) collective-permute-start(bf16[64,256]{1,0:T(8,128)(2,1)S(1)} %get-tuple-element.27.z_ref), channel_id=1, source_target_pairs={{0,384},{4,388},{8,392},{12,396},{16,400},{20,404},{48,432},{52,43... | collective-permute-start | bytes 98312 | tf_op jit(solution)/shard_map/ppermute | solution.py:179
  16.5 11.1 %collective-permute-start.1 = (bf16[64,256]{1,0:T(8,128)(2,1)S(1)}, bf16[64,256]{1,0:T(8,128)(2,1)S(1)}, u32[]{:S(2)}, u32[]{:S(2)}) collective-permute-start(bf16[64,256]{1,0:T(8,128)(2,1)S(1)} %get-tuple-element.27.z_ref), channel_id=1, source_target_pairs={{4,0},{8,4},{12,8},{16,12},{20,16},{24,20},{28,24},{32,28},{36,32}... | collective-permute-start | bytes 98312 | tf_op jit(solution)/shard_map/ppermute | solution.py:179
  27.6 0.7 %collective-permute-start = (bf16[64,256]{1,0:T(8,128)(2,1)S(1)}, bf16[64,256]{1,0:T(8,128)(2,1)S(1)}, u32[]{:S(2)}, u32[]{:S(2)}) collective-permute-start(bf16[64,256]{1,0:T(8,128)(2,1)S(1)} %get-tuple-element.27.z_ref), channel_id=1, source_target_pairs={{24,408},{28,412},{32,416},{36,420},{40,424},{44,428},{72,456},{76... | collective-permute-start | bytes 98312 | tf_op jit(solution)/shard_map/ppermute | solution.py:179
  28.3 0.7 %blocks.3 = (bf16[9,128,128]{2,1,0:T(8,128)(2,1)S(1)}, bf16[9,128,128]{2,1,0:T(8,128)(2,1)S(1)}, f32[64,256]{1,0:T(8,128)S(1)}, f32[64,1]{1,0:T(8,128)S(1)}, bf16[64,256]{1,0:T(8,128)(2,1)}) custom-call(s32[2]{0:T(128)S(1)} %copy-done.2, s32[2,32]{1,0:T(2,128)S(1)} %copy-done.3, ...), custom_call_target="tpu_custom_call", output_to_operand_aliasing={{0}: (5, {}), {1}: (6, {}), {2}: (7, {}), {3}: (8, {})} | custom-call | flops 50000000 | bytes 3145728 | tf_op jit(solution)/shard_map/blocks/pallas_call | solution.py:159
  28.9 0.0 collective-permute-done.3.before_ref
  28.9 0.0 collective-permute-done.2.first_ref
  29.0 0.2 collective-permute-done.1.after_ref
  29.2 0.0 collective-permute-done.last_ref
  29.2 0.9 %finish.1 = bf16[64,256]{1,0:T(8,128)(2,1)} custom-call(bf16[64,256]{1,0:T(8,128)(2,1)S(1)} %collective-permute-done.last_ref, bf16[64,256]{1,0:T(8,128)(2,1)S(1)} %collective-permute-done.1.after_ref, bf16[64,256]{1,0:T(8,128)(2,1)S(1)} %collective-permute-done.2.first_ref, bf16[64,256]{1,0:T(8,128)(2,1)S(1)} %collective-permute-done.3.before_ref, ...), custom_call_target="tpu_custom_call" | custom-call | tf_op jit(solution)/shard_map/finish/pallas_call | solution.py:186
Async XLA Ops:
  0.0 5.9 %copy-start = (bf16[2,32,128,128]{3,2,1,0:T(8,128)(2,1)S(1)}, bf16[2,32,128,128]{3,2,1,0:T(8,128)(2,1)}, u32[]{:S(2)}) copy-start(bf16[2,32,128,128]{3,2,1,0:T(8,128)(2,1)} %tiles_any.3) | copy-start | bytes 6291460
  0.0 5.9 %copy-start.2 = (s32[2]{0:T(128)S(1)}, s32[2]{0:T(128)}, u32[]{:S(2)}) copy-start(s32[2]{0:T(128)} %count_any.3) | copy-start | bytes 28
  0.0 5.9 %copy-start.1 = (bf16[256,64]{0,1:T(8,128)(2,1)S(1)}, bf16[256,64]{0,1:T(8,128)(2,1)}, u32[]{:S(2)}) copy-start(bf16[256,64]{0,1:T(8,128)(2,1)} %param.7) | copy-start | bytes 98308
  0.0 6.5 %copy-start.3 = (s32[2,32]{1,0:T(2,128)S(1)}, s32[2,32]{1,0:T(2,128)}, u32[]{:S(2)}) copy-start(s32[2,32]{1,0:T(2,128)} %cols_any.3) | copy-start | bytes 772
  0.0 6.5 %copy-start.4 = (f32[64]{0:T(128)S(1)}, f32[64]{0:T(128)}, u32[]{:S(2)}) copy-start(f32[64]{0:T(128)} %param.8) | copy-start | bytes 772
  7.4 21.5 %collective-permute-start.3 = (bf16[64,256]{1,0:T(8,128)(2,1)S(1)}, bf16[64,256]{1,0:T(8,128)(2,1)S(1)}, u32[]{:S(2)}, u32[]{:S(2)}) collective-permute-start(bf16[64,256]{1,0:T(8,128)(2,1)S(1)} %get-tuple-element.27.z_ref), channel_id=1, source_target_pairs={{0,4},{4,8},{8,12},{12,16},{16,20},{20,24},{24,28},{28,32},{32,36}... | collective-permute-start | bytes 98312 | tf_op jit(solution)/shard_map/ppermute | solution.py:179
  11.8 17.2 %collective-permute-start.2 = (bf16[64,256]{1,0:T(8,128)(2,1)S(1)}, bf16[64,256]{1,0:T(8,128)(2,1)S(1)}, u32[]{:S(2)}, u32[]{:S(2)}) collective-permute-start(bf16[64,256]{1,0:T(8,128)(2,1)S(1)} %get-tuple-element.27.z_ref), channel_id=1, source_target_pairs={{0,384},{4,388},{8,392},{12,396},{16,400},{20,404},{48,432},{52,43... | collective-permute-start | bytes 98312 | tf_op jit(solution)/shard_map/ppermute | solution.py:179
  16.5 12.7 %collective-permute-start.1 = (bf16[64,256]{1,0:T(8,128)(2,1)S(1)}, bf16[64,256]{1,0:T(8,128)(2,1)S(1)}, u32[]{:S(2)}, u32[]{:S(2)}) collective-permute-start(bf16[64,256]{1,0:T(8,128)(2,1)S(1)} %get-tuple-element.27.z_ref), channel_id=1, source_target_pairs={{4,0},{8,4},{12,8},{16,12},{20,16},{24,20},{28,24},{32,28},{36,32}... | collective-permute-start | bytes 98312 | tf_op jit(solution)/shard_map/ppermute | solution.py:179
  27.6 1.6 %collective-permute-start = (bf16[64,256]{1,0:T(8,128)(2,1)S(1)}, bf16[64,256]{1,0:T(8,128)(2,1)S(1)}, u32[]{:S(2)}, u32[]{:S(2)}) collective-permute-start(bf16[64,256]{1,0:T(8,128)(2,1)S(1)} %get-tuple-element.27.z_ref), channel_id=1, source_target_pairs={{24,408},{28,412},{32,416},{36,420},{40,424},{44,428},{72,456},{76... | collective-permute-start | bytes 98312 | tf_op jit(solution)/shard_map/ppermute | solution.py:179

commit v7 on v6

--- a/solution.py
+++ b/solution.py
@@ -12,7 +12,7 @@
 VMEM = pltpu.MemorySpace.VMEM
 NT = (((1,), (1,)), ((), ()))
 LINE = 12
-NEAR = 6
+NEAR = 3
 UNROLL = 3
 
 

time: 30.3 us -> 30.3 us (level)
  no operation moved by 1% of the time
where the time goes in v7:
time: 30.3 us; the launch traced here: 30.1 us
  starting transfers between devices  20.7 us (68%)
  blocking collectives  5.77 us (19%)
  Pallas kernels  3.16 us (10%)
    ppermute x4, starting transfers between devices, exchange(): lax.ppermute(z, 'row', [(s, targets(s)) for s in range(devices) if target...  20.7 us
    all_gather x1, blocking collectives, on_device(): full = lax.all_gather(panel, 'col', axis=0, tiled=True)  5.77 us
    pallas_call x2, Pallas kernels, sum_blocks(): pl.pallas_call(functools.partial(blocks_kernel, mine), out_shape=shapes,...  1.59 us
    pallas_call x1, Pallas kernels, on_device(): pl.pallas_call(finish_kernel, out_shape=jax.ShapeDtypeStruct((outs, nodes...  0.89 us
  transfers between devices with their start and end apart: 4, of which 1 were waited for; matrix products, arithmetic and copies ran while one was open for 0% of the time, Pallas kernels for 2%

profile of v7, /device:TPU:56, one launch (start us, length us, event | category | flops | bytes accessed | tf_op | source)
XLA Modules:
  0.0 30.1 jit_solution(12491505142708972158)
XLA Ops:
  0.0 0.0 copy-start
  0.0 0.0 copy-start.2
  0.0 0.0 copy-start.1
  0.0 0.0 copy-start.3
  0.0 0.0 copy-start.4
  0.0 0.1 clear.1
  0.1 5.8 %all_gather.3.full_ref = bf16[256,256]{1,0:T(8,128)(2,1)S(1)} all-gather(bf16[64,256]{1,0:T(8,128)(2,1)} %bitcast.9), channel_id=1, replica_groups=mesh['row'=192,'col'=4] {'col'}, dimensions={0}, use_global_device_ids=true | all-gather | bytes 163840 | tf_op jit(solution)/shard_map/all_gather | solution.py:127
  5.9 0.0 copy-done
  5.9 0.0 copy-done.2
  5.9 0.0 copy-done.1
  5.9 0.6 %transform.1 = (bf16[64,256]{1,0:T(8,128)(2,1)S(1)}, f32[8,256]{1,0:T(8,128)S(1)}) custom-call(s32[1,2]{1,0:T(1,128)S(1)} %bitcast.6, bf16[2,32,128,128]{3,2,1,0:T(8,128)(2,1)S(1)} %copy-done, bf16[256,256]{1,0:T(8,128)(2,1)S(1)} %all_gather.3.full_ref, bf16[64,256]{1,0:T(8,128)(2,1)S(1)} %bitcast.5), custom_call_target="tpu_custom_call" | custom-call | tf_op jit(solution)/shard_map/transform/pallas_call | solution.py:128
  6.5 0.0 copy-done.3
  6.5 0.0 copy-done.4
  6.6 0.9 %blocks.2 = (bf16[9,128,128]{2,1,0:T(8,128)(2,1)S(1)}, bf16[9,128,128]{2,1,0:T(8,128)(2,1)S(1)}, f32[64,256]{1,0:T(8,128)S(1)}, f32[64,1]{1,0:T(8,128)S(1)}, bf16[64,256]{1,0:T(8,128)(2,1)S(1)}) custom-call(s32[2]{0:T(128)S(1)} %copy-done.2, s32[2,32]{1,0:T(2,128)S(1)} %copy-done.3, ...), custom_call_target="tpu_custom_call", output_to_operand_aliasing={{0}: (5, {}), {1}: (6, {})} | custom-call | flops 50000000 | bytes 3145728 | tf_op jit(solution)/shard_map/blocks/pallas_call | solution.py:159
  7.5 4.7 %collective-permute-start.3 = (bf16[64,256]{1,0:T(8,128)(2,1)S(1)}, bf16[64,256]{1,0:T(8,128)(2,1)S(1)}, u32[]{:S(2)}, u32[]{:S(2)}) collective-permute-start(bf16[64,256]{1,0:T(8,128)(2,1)S(1)} %get-tuple-element.27.z_ref), channel_id=1, source_target_pairs={{0,4},{4,8},{8,12},{12,16},{16,20},{20,24},{24,28},{28,32},{32,36}... | collective-permute-start | bytes 98312 | tf_op jit(solution)/shard_map/ppermute | solution.py:179
  12.2 4.3 %collective-permute-start.2 = (bf16[64,256]{1,0:T(8,128)(2,1)S(1)}, bf16[64,256]{1,0:T(8,128)(2,1)S(1)}, u32[]{:S(2)}, u32[]{:S(2)}) collective-permute-start(bf16[64,256]{1,0:T(8,128)(2,1)S(1)} %get-tuple-element.27.z_ref), channel_id=1, source_target_pairs={{0,384},{4,388},{8,392},{48,432},{52,436},{56,440},{96,480},{100,4... | collective-permute-start | bytes 98312 | tf_op jit(solution)/shard_map/ppermute | solution.py:179
  16.5 11.1 %collective-permute-start.1 = (bf16[64,256]{1,0:T(8,128)(2,1)S(1)}, bf16[64,256]{1,0:T(8,128)(2,1)S(1)}, u32[]{:S(2)}, u32[]{:S(2)}) collective-permute-start(bf16[64,256]{1,0:T(8,128)(2,1)S(1)} %get-tuple-element.27.z_ref), channel_id=1, source_target_pairs={{4,0},{8,4},{12,8},{16,12},{20,16},{24,20},{28,24},{32,28},{36,32}... | collective-permute-start | bytes 98312 | tf_op jit(solution)/shard_map/ppermute | solution.py:179
  27.6 0.7 %collective-permute-start = (bf16[64,256]{1,0:T(8,128)(2,1)S(1)}, bf16[64,256]{1,0:T(8,128)(2,1)S(1)}, u32[]{:S(2)}, u32[]{:S(2)}) collective-permute-start(bf16[64,256]{1,0:T(8,128)(2,1)S(1)} %get-tuple-element.27.z_ref), channel_id=1, source_target_pairs={{12,396},{16,400},{20,404},{24,408},{28,412},{32,416},{36,420},{40... | collective-permute-start | bytes 98312 | tf_op jit(solution)/shard_map/ppermute | solution.py:179
  28.3 0.7 %blocks.3 = (bf16[9,128,128]{2,1,0:T(8,128)(2,1)S(1)}, bf16[9,128,128]{2,1,0:T(8,128)(2,1)S(1)}, f32[64,256]{1,0:T(8,128)S(1)}, f32[64,1]{1,0:T(8,128)S(1)}, bf16[64,256]{1,0:T(8,128)(2,1)}) custom-call(s32[2]{0:T(128)S(1)} %copy-done.2, s32[2,32]{1,0:T(2,128)S(1)} %copy-done.3, ...), custom_call_target="tpu_custom_call", output_to_operand_aliasing={{0}: (5, {}), {1}: (6, {}), {2}: (7, {}), {3}: (8, {})} | custom-call | flops 50000000 | bytes 3145728 | tf_op jit(solution)/shard_map/blocks/pallas_call | solution.py:159
  28.9 0.0 collective-permute-done.3.before_ref
  28.9 0.0 collective-permute-done.2.first_ref
  29.0 0.2 collective-permute-done.1.after_ref
  29.2 0.0 collective-permute-done.last_ref
  29.2 0.9 %finish.1 = bf16[64,256]{1,0:T(8,128)(2,1)} custom-call(bf16[64,256]{1,0:T(8,128)(2,1)S(1)} %collective-permute-done.last_ref, bf16[64,256]{1,0:T(8,128)(2,1)S(1)} %collective-permute-done.1.after_ref, bf16[64,256]{1,0:T(8,128)(2,1)S(1)} %collective-permute-done.2.first_ref, bf16[64,256]{1,0:T(8,128)(2,1)S(1)} %collective-permute-done.3.before_ref, ...), custom_call_target="tpu_custom_call" | custom-call | tf_op jit(solution)/shard_map/finish/pallas_call | solution.py:186
Async XLA Ops:
  0.0 5.9 %copy-start = (bf16[2,32,128,128]{3,2,1,0:T(8,128)(2,1)S(1)}, bf16[2,32,128,128]{3,2,1,0:T(8,128)(2,1)}, u32[]{:S(2)}) copy-start(bf16[2,32,128,128]{3,2,1,0:T(8,128)(2,1)} %tiles_any.3) | copy-start | bytes 6291460
  0.0 5.9 %copy-start.2 = (s32[2]{0:T(128)S(1)}, s32[2]{0:T(128)}, u32[]{:S(2)}) copy-start(s32[2]{0:T(128)} %count_any.3) | copy-start | bytes 28
  0.0 5.9 %copy-start.1 = (bf16[256,64]{0,1:T(8,128)(2,1)S(1)}, bf16[256,64]{0,1:T(8,128)(2,1)}, u32[]{:S(2)}) copy-start(bf16[256,64]{0,1:T(8,128)(2,1)} %param.7) | copy-start | bytes 98308
  0.0 6.5 %copy-start.3 = (s32[2,32]{1,0:T(2,128)S(1)}, s32[2,32]{1,0:T(2,128)}, u32[]{:S(2)}) copy-start(s32[2,32]{1,0:T(2,128)} %cols_any.3) | copy-start | bytes 772
  0.0 6.5 %copy-start.4 = (f32[64]{0:T(128)S(1)}, f32[64]{0:T(128)}, u32[]{:S(2)}) copy-start(f32[64]{0:T(128)} %param.8) | copy-start | bytes 772
  7.5 21.5 %collective-permute-start.3 = (bf16[64,256]{1,0:T(8,128)(2,1)S(1)}, bf16[64,256]{1,0:T(8,128)(2,1)S(1)}, u32[]{:S(2)}, u32[]{:S(2)}) collective-permute-start(bf16[64,256]{1,0:T(8,128)(2,1)S(1)} %get-tuple-element.27.z_ref), channel_id=1, source_target_pairs={{0,4},{4,8},{8,12},{12,16},{16,20},{20,24},{24,28},{28,32},{32,36}... | collective-permute-start | bytes 98312 | tf_op jit(solution)/shard_map/ppermute | solution.py:179
  12.2 16.8 %collective-permute-start.2 = (bf16[64,256]{1,0:T(8,128)(2,1)S(1)}, bf16[64,256]{1,0:T(8,128)(2,1)S(1)}, u32[]{:S(2)}, u32[]{:S(2)}) collective-permute-start(bf16[64,256]{1,0:T(8,128)(2,1)S(1)} %get-tuple-element.27.z_ref), channel_id=1, source_target_pairs={{0,384},{4,388},{8,392},{48,432},{52,436},{56,440},{96,480},{100,4... | collective-permute-start | bytes 98312 | tf_op jit(solution)/shard_map/ppermute | solution.py:179
  16.5 12.7 %collective-permute-start.1 = (bf16[64,256]{1,0:T(8,128)(2,1)S(1)}, bf16[64,256]{1,0:T(8,128)(2,1)S(1)}, u32[]{:S(2)}, u32[]{:S(2)}) collective-permute-start(bf16[64,256]{1,0:T(8,128)(2,1)S(1)} %get-tuple-element.27.z_ref), channel_id=1, source_target_pairs={{4,0},{8,4},{12,8},{16,12},{20,16},{24,20},{28,24},{32,28},{36,32}... | collective-permute-start | bytes 98312 | tf_op jit(solution)/shard_map/ppermute | solution.py:179
  27.6 1.6 %collective-permute-start = (bf16[64,256]{1,0:T(8,128)(2,1)S(1)}, bf16[64,256]{1,0:T(8,128)(2,1)S(1)}, u32[]{:S(2)}, u32[]{:S(2)}) collective-permute-start(bf16[64,256]{1,0:T(8,128)(2,1)S(1)} %get-tuple-element.27.z_ref), channel_id=1, source_target_pairs={{12,396},{16,400},{20,404},{24,408},{28,412},{32,416},{36,420},{40... | collective-permute-start | bytes 98312 | tf_op jit(solution)/shard_map/ppermute | solution.py:179

commit v8 on v7

--- a/solution.py
+++ b/solution.py
@@ -12,7 +12,7 @@
 VMEM = pltpu.MemorySpace.VMEM
 NT = (((1,), (1,)), ((), ()))
 LINE = 12
-NEAR = 3
+NEAR = 9
 UNROLL = 3
 
 

time: 30.3 us -> 30.3 us (level)
  no operation moved by 1% of the time
where the time goes in v8:
time: 30.3 us; the launch traced here: 30.1 us
  starting transfers between devices  20.7 us (68%)
  blocking collectives  5.77 us (19%)
  Pallas kernels  3.16 us (10%)
    ppermute x4, starting transfers between devices, exchange(): lax.ppermute(z, 'row', [(s, targets(s)) for s in range(devices) if target...  20.7 us
    all_gather x1, blocking collectives, on_device(): full = lax.all_gather(panel, 'col', axis=0, tiled=True)  5.77 us
    pallas_call x2, Pallas kernels, sum_blocks(): pl.pallas_call(functools.partial(blocks_kernel, mine), out_shape=shapes,...  1.59 us
    pallas_call x1, Pallas kernels, on_device(): pl.pallas_call(finish_kernel, out_shape=jax.ShapeDtypeStruct((outs, nodes...  0.89 us
  transfers between devices with their start and end apart: 4, of which 1 were waited for; matrix products, arithmetic and copies ran while one was open for 0% of the time, Pallas kernels for 2%

profile of v8, /device:TPU:56, one launch (start us, length us, event | category | flops | bytes accessed | tf_op | source)
XLA Modules:
  0.0 30.1 jit_solution(17635377718770225854)
XLA Ops:
  0.0 0.0 copy-start
  0.0 0.0 copy-start.2
  0.0 0.0 copy-start.1
  0.0 0.0 copy-start.3
  0.0 0.0 copy-start.4
  0.0 0.1 clear.1
  0.1 5.8 %all_gather.3.full_ref = bf16[256,256]{1,0:T(8,128)(2,1)S(1)} all-gather(bf16[64,256]{1,0:T(8,128)(2,1)} %bitcast.9), channel_id=1, replica_groups=mesh['row'=192,'col'=4] {'col'}, dimensions={0}, use_global_device_ids=true | all-gather | bytes 163840 | tf_op jit(solution)/shard_map/all_gather | solution.py:127
  5.9 0.0 copy-done
  5.9 0.0 copy-done.2
  5.9 0.0 copy-done.1
  5.9 0.6 %transform.1 = (bf16[64,256]{1,0:T(8,128)(2,1)S(1)}, f32[8,256]{1,0:T(8,128)S(1)}) custom-call(s32[1,2]{1,0:T(1,128)S(1)} %bitcast.6, bf16[2,32,128,128]{3,2,1,0:T(8,128)(2,1)S(1)} %copy-done, bf16[256,256]{1,0:T(8,128)(2,1)S(1)} %all_gather.3.full_ref, bf16[64,256]{1,0:T(8,128)(2,1)S(1)} %bitcast.5), custom_call_target="tpu_custom_call" | custom-call | tf_op jit(solution)/shard_map/transform/pallas_call | solution.py:128
  6.5 0.0 copy-done.3
  6.5 0.0 copy-done.4
  6.6 0.9 %blocks.2 = (bf16[9,128,128]{2,1,0:T(8,128)(2,1)S(1)}, bf16[9,128,128]{2,1,0:T(8,128)(2,1)S(1)}, f32[64,256]{1,0:T(8,128)S(1)}, f32[64,1]{1,0:T(8,128)S(1)}, bf16[64,256]{1,0:T(8,128)(2,1)S(1)}) custom-call(s32[2]{0:T(128)S(1)} %copy-done.2, s32[2,32]{1,0:T(2,128)S(1)} %copy-done.3, ...), custom_call_target="tpu_custom_call", output_to_operand_aliasing={{0}: (5, {}), {1}: (6, {})} | custom-call | flops 50000000 | bytes 3145728 | tf_op jit(solution)/shard_map/blocks/pallas_call | solution.py:159
  7.5 4.7 %collective-permute-start.3 = (bf16[64,256]{1,0:T(8,128)(2,1)S(1)}, bf16[64,256]{1,0:T(8,128)(2,1)S(1)}, u32[]{:S(2)}, u32[]{:S(2)}) collective-permute-start(bf16[64,256]{1,0:T(8,128)(2,1)S(1)} %get-tuple-element.27.z_ref), channel_id=1, source_target_pairs={{0,4},{4,8},{8,12},{12,16},{16,20},{20,24},{24,28},{28,32},{32,36}... | collective-permute-start | bytes 98312 | tf_op jit(solution)/shard_map/ppermute | solution.py:179
  12.2 4.3 %collective-permute-start.2 = (bf16[64,256]{1,0:T(8,128)(2,1)S(1)}, bf16[64,256]{1,0:T(8,128)(2,1)S(1)}, u32[]{:S(2)}, u32[]{:S(2)}) collective-permute-start(bf16[64,256]{1,0:T(8,128)(2,1)S(1)} %get-tuple-element.27.z_ref), channel_id=1, source_target_pairs={{0,384},{4,388},{8,392},{12,396},{16,400},{20,404},{24,408},{28,41... | collective-permute-start | bytes 98312 | tf_op jit(solution)/shard_map/ppermute | solution.py:179
  16.5 11.1 %collective-permute-start.1 = (bf16[64,256]{1,0:T(8,128)(2,1)S(1)}, bf16[64,256]{1,0:T(8,128)(2,1)S(1)}, u32[]{:S(2)}, u32[]{:S(2)}) collective-permute-start(bf16[64,256]{1,0:T(8,128)(2,1)S(1)} %get-tuple-element.27.z_ref), channel_id=1, source_target_pairs={{4,0},{8,4},{12,8},{16,12},{20,16},{24,20},{28,24},{32,28},{36,32}... | collective-permute-start | bytes 98312 | tf_op jit(solution)/shard_map/ppermute | solution.py:179
  27.6 0.7 %collective-permute-start = (bf16[64,256]{1,0:T(8,128)(2,1)S(1)}, bf16[64,256]{1,0:T(8,128)(2,1)S(1)}, u32[]{:S(2)}, u32[]{:S(2)}) collective-permute-start(bf16[64,256]{1,0:T(8,128)(2,1)S(1)} %get-tuple-element.27.z_ref), channel_id=1, source_target_pairs={{36,420},{40,424},{44,428},{84,468},{88,472},{92,476},{132,516},{1... | collective-permute-start | bytes 98312 | tf_op jit(solution)/shard_map/ppermute | solution.py:179
  28.3 0.7 %blocks.3 = (bf16[9,128,128]{2,1,0:T(8,128)(2,1)S(1)}, bf16[9,128,128]{2,1,0:T(8,128)(2,1)S(1)}, f32[64,256]{1,0:T(8,128)S(1)}, f32[64,1]{1,0:T(8,128)S(1)}, bf16[64,256]{1,0:T(8,128)(2,1)}) custom-call(s32[2]{0:T(128)S(1)} %copy-done.2, s32[2,32]{1,0:T(2,128)S(1)} %copy-done.3, ...), custom_call_target="tpu_custom_call", output_to_operand_aliasing={{0}: (5, {}), {1}: (6, {}), {2}: (7, {}), {3}: (8, {})} | custom-call | flops 50000000 | bytes 3145728 | tf_op jit(solution)/shard_map/blocks/pallas_call | solution.py:159
  28.9 0.0 collective-permute-done.3.before_ref
  28.9 0.0 collective-permute-done.2.first_ref
  29.0 0.2 collective-permute-done.1.after_ref
  29.2 0.0 collective-permute-done.last_ref
  29.2 0.9 %finish.1 = bf16[64,256]{1,0:T(8,128)(2,1)} custom-call(bf16[64,256]{1,0:T(8,128)(2,1)S(1)} %collective-permute-done.last_ref, bf16[64,256]{1,0:T(8,128)(2,1)S(1)} %collective-permute-done.1.after_ref, bf16[64,256]{1,0:T(8,128)(2,1)S(1)} %collective-permute-done.2.first_ref, bf16[64,256]{1,0:T(8,128)(2,1)S(1)} %collective-permute-done.3.before_ref, ...), custom_call_target="tpu_custom_call" | custom-call | tf_op jit(solution)/shard_map/finish/pallas_call | solution.py:186
Async XLA Ops:
  0.0 5.9 %copy-start = (bf16[2,32,128,128]{3,2,1,0:T(8,128)(2,1)S(1)}, bf16[2,32,128,128]{3,2,1,0:T(8,128)(2,1)}, u32[]{:S(2)}) copy-start(bf16[2,32,128,128]{3,2,1,0:T(8,128)(2,1)} %tiles_any.3) | copy-start | bytes 6291460
  0.0 5.9 %copy-start.2 = (s32[2]{0:T(128)S(1)}, s32[2]{0:T(128)}, u32[]{:S(2)}) copy-start(s32[2]{0:T(128)} %count_any.3) | copy-start | bytes 28
  0.0 5.9 %copy-start.1 = (bf16[256,64]{0,1:T(8,128)(2,1)S(1)}, bf16[256,64]{0,1:T(8,128)(2,1)}, u32[]{:S(2)}) copy-start(bf16[256,64]{0,1:T(8,128)(2,1)} %param.7) | copy-start | bytes 98308
  0.0 6.5 %copy-start.3 = (s32[2,32]{1,0:T(2,128)S(1)}, s32[2,32]{1,0:T(2,128)}, u32[]{:S(2)}) copy-start(s32[2,32]{1,0:T(2,128)} %cols_any.3) | copy-start | bytes 772
  0.0 6.5 %copy-start.4 = (f32[64]{0:T(128)S(1)}, f32[64]{0:T(128)}, u32[]{:S(2)}) copy-start(f32[64]{0:T(128)} %param.8) | copy-start | bytes 772
  7.5 21.5 %collective-permute-start.3 = (bf16[64,256]{1,0:T(8,128)(2,1)S(1)}, bf16[64,256]{1,0:T(8,128)(2,1)S(1)}, u32[]{:S(2)}, u32[]{:S(2)}) collective-permute-start(bf16[64,256]{1,0:T(8,128)(2,1)S(1)} %get-tuple-element.27.z_ref), channel_id=1, source_target_pairs={{0,4},{4,8},{8,12},{12,16},{16,20},{20,24},{24,28},{28,32},{32,36}... | collective-permute-start | bytes 98312 | tf_op jit(solution)/shard_map/ppermute | solution.py:179
  12.2 16.8 %collective-permute-start.2 = (bf16[64,256]{1,0:T(8,128)(2,1)S(1)}, bf16[64,256]{1,0:T(8,128)(2,1)S(1)}, u32[]{:S(2)}, u32[]{:S(2)}) collective-permute-start(bf16[64,256]{1,0:T(8,128)(2,1)S(1)} %get-tuple-element.27.z_ref), channel_id=1, source_target_pairs={{0,384},{4,388},{8,392},{12,396},{16,400},{20,404},{24,408},{28,41... | collective-permute-start | bytes 98312 | tf_op jit(solution)/shard_map/ppermute | solution.py:179
  16.5 12.7 %collective-permute-start.1 = (bf16[64,256]{1,0:T(8,128)(2,1)S(1)}, bf16[64,256]{1,0:T(8,128)(2,1)S(1)}, u32[]{:S(2)}, u32[]{:S(2)}) collective-permute-start(bf16[64,256]{1,0:T(8,128)(2,1)S(1)} %get-tuple-element.27.z_ref), channel_id=1, source_target_pairs={{4,0},{8,4},{12,8},{16,12},{20,16},{24,20},{28,24},{32,28},{36,32}... | collective-permute-start | bytes 98312 | tf_op jit(solution)/shard_map/ppermute | solution.py:179
  27.6 1.6 %collective-permute-start = (bf16[64,256]{1,0:T(8,128)(2,1)S(1)}, bf16[64,256]{1,0:T(8,128)(2,1)S(1)}, u32[]{:S(2)}, u32[]{:S(2)}) collective-permute-start(bf16[64,256]{1,0:T(8,128)(2,1)S(1)} %get-tuple-element.27.z_ref), channel_id=1, source_target_pairs={{36,420},{40,424},{44,428},{84,468},{88,472},{92,476},{132,516},{1... | collective-permute-start | bytes 98312 | tf_op jit(solution)/shard_map/ppermute | solution.py:179
